TPU v7x, 1024 devices: a whole 8x8x8 slice. The times are simulated.
1024 devices in a mesh: wave: 16 (over z, core), lev: 64 (over x, y).
Axes of the slice: x: 8, y: 8, z: 8, core: 2. Of those that a mesh axis runs over, the one named last changes fastest.
Arguments:
- grid_values: bfloat16 [256, 480, 1024], P('lev', 'wave'), may hold values from -6 to 6
- legendre: bfloat16 [160, 480, 384], P('wave'), as said below
- gauss_weights: float32 [480], replicated, may hold values from 0.5 to 1.5
- modes_in: bfloat16 [128, 128], replicated, may hold values from -0.5 to 0.5
- modes_out: bfloat16 [128, 128], replicated, may hold values from -0.5 to 0.5
- stiffness: float32 [128], replicated, may hold values from 0.1 to 10
- slot_pair: int32 [160], replicated, may hold values from 0 to 159, each once
- lat_order: int32 [480], replicated, may hold values from 0 to 479, each once
- field_slots: int32 [256], replicated, may hold values from 0 to 255, each once
Outputs:
- product: bfloat16 [256, 480, 1024], P('lev', 'wave')
Inputs may be any that keep to these rules, and one draw needn't show every extreme that they name: legendre is zero in every column c > 320. `slot_pair`: a permutation. `lat_order`: a permutation. `field_slots`: a permutation.
All inputs are finite; a program needn't handle non-finite values.
Results may differ from a plain program's by a relative error of at most 0.0085.
Values may be sent and summed in bfloat16 or wider, within the bound.
A program may use at most 32 MiB of HBM per device.

v0:
```python
import jax
import jax.numpy as jnp
from jax import lax
from jax.sharding import PartitionSpec as P

NM = 320
LEVELS = 128


def fourier_table(wavenumbers, longitudes):
    lon_index = jnp.arange(longitudes, dtype=jnp.int32)
    phase_steps = lon_index[:, None] * wavenumbers[None, :] % longitudes
    angles = phase_steps.astype(jnp.float32) * (2.0 * jnp.pi / longitudes)
    scaling = 1.0 / jnp.sqrt(jnp.float32(longitudes))
    entries = jnp.stack([jnp.cos(angles), -jnp.sin(angles)], axis=2) * scaling
    return entries.astype(jnp.bfloat16).reshape(longitudes, 2 * wavenumbers.shape[0])


def paired_waves(slot_pair):
    return jnp.stack([slot_pair, NM - 1 - slot_pair], axis=1).reshape(-1)


def local(
    grid_values,
    legendre,
    gauss_weights,
    modes_in,
    modes_out,
    stiffness,
    slot_pair,
    lat_order,
    field_slots,
):
    row_count, lat_local, lon_count = grid_values.shape
    slot_local, lat_count, column_count = legendre.shape
    lev_size = lax.axis_size("lev")
    wave_rank = lax.axis_index("wave")
    lev_rank = lax.axis_index("lev")
    wave_table = fourier_table(paired_waves(slot_pair), lon_count)
    own_lats = lax.dynamic_slice_in_dim(lat_order, wave_rank * lat_local, lat_local)
    row_weight = gauss_weights[own_lats]
    own_pairs = lax.dynamic_slice_in_dim(slot_pair, wave_rank * slot_local, slot_local)
    column = jnp.arange(column_count, dtype=jnp.int32)
    first_half = column[None, :] < (NM - own_pairs)[:, None]
    keep_mask = first_half[None, :, None, :]
    block_rows = grid_values.shape[0]
    fourier = jnp.dot(
        grid_values.reshape(block_rows * lat_local, lon_count),
        wave_table,
        preferred_element_type=jnp.float32,
    )
    fourier = (fourier.reshape(block_rows, lat_local, -1) * row_weight[None, :, None]).astype(
        jnp.bfloat16
    )
    arrived = lax.all_to_all(fourier, "wave", split_axis=2, concat_axis=1, tiled=True)
    true_order = jnp.zeros_like(arrived).at[:, lat_order].set(arrived)
    grouped = true_order.reshape(block_rows, lat_count, slot_local, 2, 2)
    both_waves = jnp.einsum(
        "fjkar,kjc->afkrc", grouped, legendre, preferred_element_type=jnp.float32
    )
    spectral = jnp.where(keep_mask, both_waves[0], both_waves[1]).astype(jnp.bfloat16)
    flattened = spectral.reshape(row_count, slot_local * 2 * column_count)
    gathered = lax.all_to_all(flattened, "lev", split_axis=1, concat_axis=0, tiled=True)
    share_width = flattened.shape[1] // lev_size
    positions = lev_rank * share_width + jnp.arange(share_width, dtype=jnp.int32)
    slot_index = positions // (2 * column_count)
    column_index = positions % column_count
    pair_values = own_pairs[slot_index]
    degree = jnp.where(
        column_index < NM - pair_values, pair_values + column_index, column_index - 1
    ).astype(jnp.float32)
    growth = degree * (degree + 1.0) / (NM * NM)
    factor = 1.0 / (1.0 + growth[None, :] * stiffness[:, None])
    ordered = jnp.zeros_like(gathered).at[field_slots].set(gathered)
    fields_count = gathered.shape[0] // LEVELS
    stacked = ordered.reshape(fields_count, LEVELS, share_width)
    projected = jnp.einsum("ml,fls->fms", modes_in, stacked, preferred_element_type=jnp.float32)
    modal_values = (projected * factor[None]).astype(jnp.bfloat16)
    restored = jnp.einsum(
        "lm,fms->fls", modes_out, modal_values, preferred_element_type=jnp.float32
    ).astype(jnp.bfloat16)
    implicit = restored.reshape(-1, share_width)[field_slots]
    returned = lax.all_to_all(implicit, "lev", split_axis=0, concat_axis=1, tiled=True)
    coefficients = returned.reshape(row_count, slot_local, 2, column_count)
    block_rows = coefficients.shape[0]
    empty_coeff = jnp.zeros_like(coefficients)
    split_waves = jnp.stack(
        [
            jnp.where(keep_mask, coefficients, empty_coeff),
            jnp.where(keep_mask, empty_coeff, coefficients),
        ],
        axis=0,
    )
    fourier_back = jnp.einsum(
        "afkrc,kjc->fjkar", split_waves, legendre, preferred_element_type=jnp.float32
    ).astype(jnp.bfloat16)
    back_rows = fourier_back[:, lat_order].reshape(block_rows, lat_count, slot_local * 4)
    arrived = lax.all_to_all(back_rows, "wave", split_axis=1, concat_axis=2, tiled=True)
    field_values = lax.dot_general(
        arrived.reshape(block_rows * lat_local, -1),
        wave_table,
        (((1,), (1,)), ((), ())),
        preferred_element_type=jnp.float32,
    )
    product = field_values.reshape(block_rows, lat_local, lon_count) * grid_values.astype(
        jnp.float32
    )
    return product.astype(jnp.bfloat16)


def solution(mesh):
    in_specs = (P("lev", "wave", None), P("wave", None, None), P(), P(), P(), P(), P(), P(), P())
    out_specs = P("lev", "wave", None)
    return jax.shard_map(local, mesh=mesh, in_specs=in_specs, out_specs=out_specs, check_vma=False)
```

profile of v0, /device:TPU:1, one launch (start us, length us, event | category | flops | bytes accessed | tf_op | source)
XLA Modules:
  0.0 140.0 jit_solution(6754353023368801438)
XLA Ops:
  0.0 0.7 broadcast_subtract_fusion
  0.7 0.8 compare_select_fusion.3
  1.5 0.7 pad_add_fusion
  2.3 0.1 mul.115
  2.4 1.0 copy.155
  3.5 5.2 %fusion.31 = (f32[1024,320,1]{0,1,2:T(8,128)S(1)}, f32[1024,320,1]{0,1,2:T(8,128)S(1)}) fusion(s32[320]{0:T(512)S(1)} %mul.115), kind=kLoop, calls=%fused_computation.35 | loop fusion | flops 4915200 | bytes 2622720 | tf_op jit(solution)/shard_map/cos | solution.py:15
  8.8 0.3 fusion.4
  9.1 1.3 copy.154
  10.5 0.5 convert_element_type.69
  11.0 0.5 convolution_bitcast_fusion
  11.7 0.7 gather_fusion
  12.5 0.4 copy.156
  12.9 1.5 %reshape.412 = bf16[16,2,2400]{2,1,0:T(2,128)(2,1)} reshape(bf16[640,4,30]{2,1,0:T(4,128)(2,1)S(1)} %bitcast.120) | data formatting | bytes 307200
  14.4 18.2 %all-to-all-start = ((bf16[16,2,2400]{2,1,0:T(2,128)(2,1)}), bf16[16,2,2400]{2,1,0:T(2,128)(2,1)S(1)}, u32[]{:S(2)}, u32[]{:S(2)}) async-start(bf16[16,2,2400]{2,1,0:T(2,128)(2,1)} %reshape.412), calls=%async_computation | async-start | bytes 311296 | tf_op jit(solution)/shard_map/all_to_all | solution.py:55
  32.7 0.7 fusion.47
  33.6 6.3 %fusion.42 = f32[120]{0:T(128)S(1)} fusion(s32[]{:T(128)} %bitcast.22, s32[]{:T(128)} %bitcast.23, s32[]{:T(128)} %bitcast.24, s32[]{:T(128)} %bitcast.25, s32[]{:T(128)} %bitcast.26, s32[]{:T(128)} %bitcast.28, s32[]{:T(128)} %bitcast.27, s32[]{:T(128)} %bitcast.17, s32[]{:T(128)} %bitcast.19, s32[]{:T(128)} %bitcast.21, s32[]{:T(128)S(6)} %mul.125), kind=kLoop, calls=%fused_computation.73 | loop fusion | flops 5520 | bytes 524 | tf_op jit(solution)/shard_map/div | solution.py:72
  40.0 2.0 %all-to-all-done = bf16[16,2,2400]{2,1,0:T(2,128)(2,1)S(1)} async-done(((bf16[16,2,2400]{2,1,0:T(2,128)(2,1)}), bf16[16,2,2400]{2,1,0:T(2,128)(2,1)S(1)}, u32[]{:S(2)}, u32[]{:S(2)}) %all-to-all-start) | async-done | bytes 153632 | tf_op jit(solution)/shard_map/all_to_all | solution.py:55
  42.0 1.0 reshape.413
  43.1 0.3 copy.198
  43.3 0.6 reshape.353
  44.0 0.3 copy.159
  44.2 0.1 broadcast_in_dim.58
  44.4 14.9 %scatter_fusion = bf16[4,480,40]{2,0,1:T(4,128)(2,1)S(1)} fusion(bf16[4,480,40]{2,0,1:T(4,128)(2,1)S(1)} %broadcast_in_dim.58, s32[480]{0:T(512)S(1)} %compare_select_fusion, bf16[480,4,40]{2,1,0:T(4,128)(2,1)S(1)} %copy.159), kind=kCustom, calls=%fused_computation.3 | custom fusion | bytes 462720 | tf_op jit(solution)/shard_map/scatter | solution.py:56
  59.3 0.3 copy.160
  59.6 2.7 %fusion.19 = bf16[2,4,10,2,384]{4,1,3,0,2:T(4,128)(2,1)S(1)} fusion(bf16[4,480,10,2,2]{1,0,4,3,2:T(4,128)(2,1)S(1)} %bitcast.126, bf16[10,480,384]{2,1,0:T(8,128)(2,1)} %param.10), kind=kOutput, calls=%fused_computation.26 | convolution fusion | flops 58982400 | bytes 3962880 | tf_op jit(solution)/shard_map/fjkar,kjc->afkrc/dot_general | solution.py:58
  62.5 0.2 squeeze.7
  62.7 0.2 squeeze.6
  62.9 0.7 copy.163
  63.6 13.2 %all-to-all-start.1 = ((bf16[4,64,120]{2,0,1:T(4,128)(2,1)}), bf16[4,64,120]{2,0,1:T(4,128)(2,1)S(1)}, u32[]{:S(2)}, u32[]{:S(2)}) async-start(bf16[4,64,120]{2,0,1:T(4,128)(2,1)} %copy.163), calls=%async_computation.1 | async-start | bytes 131072 | tf_op jit(solution)/shard_map/all_to_all | solution.py:63
  76.9 11.1 %all-to-all-done.1 = bf16[4,64,120]{2,0,1:T(4,128)(2,1)S(1)} async-done(((bf16[4,64,120]{2,0,1:T(4,128)(2,1)}), bf16[4,64,120]{2,0,1:T(4,128)(2,1)S(1)}, u32[]{:S(2)}, u32[]{:S(2)}) %all-to-all-start.1) | async-done | bytes 61472 | tf_op jit(solution)/shard_map/all_to_all | solution.py:63
  87.9 1.2 scatter_custom_fusion.1
  89.1 0.4 fusion.30
  89.5 0.1 copy.186
  89.6 1.5 %gather_fusion.1 = bf16[256,120]{1,0:T(8,128)(2,1)} fusion(bf16[256,120]{1,0:T(8,128)(2,1)S(1)} %bitcast.119, s32[1024]{0:T(1024)S(1)} %pad_clamp_fusion.1), kind=kCustom, calls=%fused_computation.1 | custom fusion | bytes 123904 | tf_op jit(solution)/shard_map/gather | solution.py:82
  91.1 4.6 %all-to-all-start.2 = ((bf16[64,4,120]{2,1,0:T(4,128)(2,1)}), bf16[64,4,120]{2,1,0:T(4,128)(2,1)S(1)}, u32[]{:S(2)}, u32[]{:S(2)}) async-start(bf16[64,4,120]{2,1,0:T(4,128)(2,1)} %bitcast.33), calls=%async_computation.2 | async-start | bytes 131072 | tf_op jit(solution)/shard_map/all_to_all | solution.py:83
  95.8 11.1 %all-to-all-done.2 = bf16[64,4,120]{2,1,0:T(4,128)(2,1)S(1)} async-done(((bf16[64,4,120]{2,1,0:T(4,128)(2,1)}), bf16[64,4,120]{2,1,0:T(4,128)(2,1)S(1)}, u32[]{:S(2)}, u32[]{:S(2)}) %all-to-all-start.2) | async-done | bytes 61472 | tf_op jit(solution)/shard_map/all_to_all | solution.py:83
  106.8 0.2 reshape.309
  107.1 3.3 %fusion.25 = bf16[4,480,10,2,2]{1,0,4,3,2:T(4,128)(2,1)S(1)} fusion(bf16[10,480,384]{2,1,0:T(8,128)(2,1)} %param.10, bf16[1,4,10,2,384]{4,1,3,0,2:T(4,128)(2,1)S(1)} %get-tuple-element.10, bf16[1,4,10,2,384]{4,1,3,0,2:T(4,128)(2,1)S(1)} %get-tuple-element.9), kind=kOutput, calls=%fused_computation.28 | convolution fusion | flops 59304960 | bytes 3962880 | tf_op jit(solution)/shard_map/afkrc,kjc->fjkar/dot_general | solution.py:94
  110.4 1.8 %copy.171 = bf16[4,480,10,2,2]{2,0,4,3,1:T(4,128)(2,1)S(1)} copy(bf16[4,480,10,2,2]{1,0,4,3,2:T(4,128)(2,1)S(1)} %fusion.25) | data formatting | bytes 307200 | tf_op jit(solution)/shard_map/convert_element_type | solution.py:96
  112.2 3.8 %gather_fusion.2 = bf16[480,4,10,2,2]{2,1,4,3,0:T(4,128)(2,1)} fusion(bf16[4,480,10,2,2]{2,0,4,3,1:T(4,128)(2,1)S(1)} %copy.171, s32[1024]{0:T(1024)S(1)} %pad_clamp_fusion), kind=kCustom, calls=%fused_computation.2 | custom fusion | bytes 309120 | tf_op jit(solution)/shard_map/gather | solution.py:97
  116.0 3.2 %copy.172 = bf16[4,480,10,2,2]{1,0,4,3,2:T(4,128)(2,1)S(1)} copy(bf16[4,480,10,2,2]{2,0,4,3,1:T(4,128)(2,1)} %bitcast.118) | data formatting | bytes 307200 | tf_op jit(solution)/shard_map/gather | solution.py:97
  119.3 0.3 copy.173
  119.6 0.7 reshape.414
  120.3 17.1 %all_to_all.65 = bf16[16,2,2400]{2,1,0:T(2,128)(2,1)S(1)} all-to-all(bf16[16,2,2400]{2,1,0:T(2,128)(2,1)S(1)} %reshape.414), channel_id=1, replica_groups=mesh['wave'=16,'lev'=64] {'wave'}, dimensions={0} | all-to-all | bytes 307200 | tf_op jit(solution)/shard_map/all_to_all | solution.py:98
  137.4 0.6 reshape.415
  138.1 0.6 dot_general.28
  138.7 0.4 fusion.16
  139.1 0.9 copy.179
  (37 shorter events, 1.2 us)
Async XLA Ops:
  0.0 89.1 %copy-start = (bf16[128,128]{1,0:T(8,128)(2,1)S(1)}, bf16[128,128]{1,0:T(8,128)(2,1)}, u32[]{:S(2)}) copy-start(bf16[128,128]{1,0:T(8,128)(2,1)} %param.13) | copy-start | bytes 98308
  11.0 0.7 copy-start.1
  12.4 20.2 %copy-start.5 = (s32[480]{0:T(512)S(1)}, s32[480]{0:T(512)}, u32[]{:S(2)}) copy-start(s32[480]{0:T(512)} %param.16) | copy-start | bytes 5764
  12.4 20.3 %copy-start.4 = (s32[160]{0:T(256)S(1)}, s32[160]{0:T(256)}, u32[]{:S(2)}) copy-start(s32[160]{0:T(256)} %param.15) | copy-start | bytes 1924
  12.4 27.5 %copy-start.7 = (f32[128]{0:T(128)S(1)}, f32[128]{0:T(128)}, u32[]{:S(2)}) copy-start(f32[128]{0:T(128)} %param.14) | copy-start | bytes 1540
  14.4 27.6 %all-to-all-start = ((bf16[16,2,2400]{2,1,0:T(2,128)(2,1)}), bf16[16,2,2400]{2,1,0:T(2,128)(2,1)S(1)}, u32[]{:S(2)}, u32[]{:S(2)}) async-start(bf16[16,2,2400]{2,1,0:T(2,128)(2,1)} %reshape.412), calls=%async_computation | async-start | bytes 311296 | tf_op jit(solution)/shard_map/all_to_all | solution.py:55
  59.6 17.2 %copy-start.6 = (s32[256]{0:T(256)S(1)}, s32[256]{0:T(256)}, u32[]{:S(2)}) copy-start(s32[256]{0:T(256)} %param.17) | copy-start | bytes 3076
  62.4 26.8 %copy-start.3 = (bf16[128,128]{1,0:T(8,128)(2,1)S(1)}, bf16[128,128]{1,0:T(8,128)(2,1)}, u32[]{:S(2)}) copy-start(bf16[128,128]{1,0:T(8,128)(2,1)} %param.12) | copy-start | bytes 98308
  63.6 24.3 %all-to-all-start.1 = ((bf16[4,64,120]{2,0,1:T(4,128)(2,1)}), bf16[4,64,120]{2,0,1:T(4,128)(2,1)S(1)}, u32[]{:S(2)}, u32[]{:S(2)}) async-start(bf16[4,64,120]{2,0,1:T(4,128)(2,1)} %copy.163), calls=%async_computation.1 | async-start | bytes 131072 | tf_op jit(solution)/shard_map/all_to_all | solution.py:63
  91.1 15.7 %all-to-all-start.2 = ((bf16[64,4,120]{2,1,0:T(4,128)(2,1)}), bf16[64,4,120]{2,1,0:T(4,128)(2,1)S(1)}, u32[]{:S(2)}, u32[]{:S(2)}) async-start(bf16[64,4,120]{2,1,0:T(4,128)(2,1)} %bitcast.33), calls=%async_computation.2 | async-start | bytes 131072 | tf_op jit(solution)/shard_map/all_to_all | solution.py:83
  120.3 18.4 %copy-start.2 = (bf16[4,30,1024]{2,0,1:T(4,128)(2,1)S(1)}, bf16[4,30,1024]{2,0,1:T(4,128)(2,1)}, u32[]{:S(2)}) copy-start(bf16[4,30,1024]{2,0,1:T(4,128)(2,1)} %param.9) | copy-start | bytes 737284
where the time goes:
time: 141 us; the launch traced here: 140 us
  local copies, waits for them, and re-layouts  40.5 us (29%)
  starting transfers between devices  36 us (26%)
  waiting for transfers between devices  24.2 us (17%)
  blocking collectives  17.1 us (12%)
  other arithmetic  14.4 us (10%)
  matrix products  7.32 us (5%)
    all_to_all x1, starting transfers between devices, local(): lax.all_to_all(fourier, 'wave', split_axis=2, concat_axis=1, tiled=True)  18.2 us
    all_to_all x1, blocking collectives, local(): lax.all_to_all(back_rows, 'wave', split_axis=1, concat_axis=2, tiled=True)  17.1 us
    scatter x2, local copies, waits for them, and re-layouts, local(): true_order = jnp.zeros_like(arrived).at[:, lat_order].set(arrived)  15.2 us
    all_to_all x1, starting transfers between devices, local(): lax.all_to_all(flattened, 'lev', split_axis=1, concat_axis=0, tiled=True)  13.2 us
    all_to_all x1, waiting for transfers between devices, local(): lax.all_to_all(flattened, 'lev', split_axis=1, concat_axis=0, tiled=True)  11.1 us
    all_to_all x1, waiting for transfers between devices, local(): lax.all_to_all(implicit, 'lev', split_axis=0, concat_axis=1, tiled=True)  11.1 us
    gather x2, local copies, waits for them, and re-layouts, local(): fourier_back[:, lat_order].reshape(block_rows, lat_count, slot_local * 4)  7.01 us
    div x1, other arithmetic, local(): growth = degree * (degree + 1.0) / (NM * NM)  6.25 us
  transfers between devices with their start and end apart: 3, of which 3 were waited for; matrix products, arithmetic and copies ran while one was open for 5% of the time, Pallas kernels for 0%

commit v1 on v0

v1 whole, which is shorter than its diff:
```python
import functools

import jax
import jax.numpy as jnp
import numpy as np
from jax import lax
from jax.experimental import pallas as pl
from jax.experimental.pallas import tpu as pltpu
from jax.sharding import PartitionSpec as P

NM = 320
LEVELS = 128
W = 16
LV = 64
ROWS = 4
JL = 30
JP = 32
SLOTS = 10
LAT = 480
COLS = 384
NB = 60
NLON = 1024
F32 = jnp.float32
BF16 = jnp.bfloat16
MESH = pl.DeviceIdType.MESH
HBM = pl.BlockSpec(memory_space=pltpu.HBM)
VMEM = pl.BlockSpec(memory_space=pltpu.VMEM)
SMEM = pl.BlockSpec(memory_space=pltpu.SMEM)
DMA = pltpu.SemaphoreType.DMA


def fourier_rows():
    steps = (np.arange(NM)[:, None] * np.arange(NLON)[None, :]) % NLON
    angles = steps.astype(np.float32) * np.float32(2.0 * np.pi / NLON)
    entries = np.stack([np.cos(angles), -np.sin(angles)], axis=1) / np.float32(32.0)
    return entries.reshape(2 * NM, NLON).astype(jnp.bfloat16)


def iota(shape, axis):
    return lax.broadcasted_iota(jnp.int32, shape, axis)


def one_hot(condition):
    return jnp.where(condition, 1.0, 0.0).astype(F32).astype(BF16)


def dot(a, b):
    return jnp.dot(a, b, preferred_element_type=F32)


def dot_nt(a, b):
    return lax.dot_general(a, b, (((1,), (1,)), ((), ())), preferred_element_type=F32)


def signal_axis(axis, size):
    me = lax.axis_index(axis)
    barrier = pltpu.get_barrier_semaphore()

    def send(i, carry):
        pl.semaphore_signal(
            barrier, inc=1, device_id={axis: lax.rem(me + i, size)}, device_id_type=MESH
        )
        return carry

    lax.fori_loop(1, size, send, 0)


def wait_axis(size):
    pl.semaphore_wait(pltpu.get_barrier_semaphore(), size - 1)


def lat_selector(lat_ref):
    lat = lat_ref[...]
    j = iota((LAT, W * JP), 0)
    jp = iota((LAT, W * JP), 1)
    local = jp & (JP - 1)
    spread = one_hot((j == (jp >> 5) * JL + local) & (local < JL))
    high = jnp.broadcast_to((lat >> 5).astype(F32), (8, LAT)).astype(BF16)
    low = jnp.broadcast_to((lat & 31).astype(F32), (8, LAT)).astype(BF16)
    there = dot(high, spread)[0:1] * 32.0 + dot(low, spread)[0:1]
    there = jnp.where((iota((1, W * JP), 1) & (JP - 1)) < JL, there, -1.0)
    return one_hot(iota((LAT, W * JP), 0).astype(F32) == there)


def rows_to_lanes(pieces):
    return [
        jnp.concatenate([piece[:, JP * b : JP * b + JP] for piece in pieces], axis=1)
        for b in range(4)
    ]


def load_grid(grid_ref, spread):
    spread[...] = jnp.zeros_like(spread)
    for jl in range(JL):
        rows = grid_ref[jl].astype(F32)
        for b in range(8):
            spread[b, pl.ds(jl, ROWS, stride=JP), :] = rows[:, 128 * b : 128 * b + 128]


def joined(ref):
    return jnp.concatenate([ref[b] for b in range(ref.shape[0])], axis=1)


def exchange_wave(send_buf, recv_buf, send_sem, recv_sem):
    w = lax.axis_index("wave")

    def send(i, carry):
        to = lax.rem(w + i, W)
        pltpu.make_async_remote_copy(
            src_ref=send_buf.at[to],
            dst_ref=recv_buf.at[w],
            send_sem=send_sem,
            recv_sem=recv_sem,
            device_id={"wave": to},
            device_id_type=MESH,
        ).start()
        return carry

    lax.fori_loop(1, W, send, 0)
    recv_buf[w] = send_buf[w]


def wait_bytes(ref, count, sem):
    part = ref.at[pl.ds(0, count)]
    pltpu.make_async_copy(part, part, sem).wait()


def kernel_a(
    lat_s, gauss_s, lat_ref, pair_ref, grid_hbm, table_hbm, out_ref,
    grid_v, table_v, spread, send_buf, recv_buf, mixed, copy_sem, send_sem, recv_sem,
):
    w = lax.axis_index("wave")
    signal_axis("wave", W)
    get_grid = pltpu.make_async_copy(grid_hbm, grid_v, copy_sem.at[0])
    get_table = pltpu.make_async_copy(table_hbm, table_v, copy_sem.at[1])
    get_grid.start()
    get_table.start()

    lane = iota((1, 128), 1)

    def add_weight(jl, weight):
        value = gauss_s[lat_s[w * JL + jl]]
        return jnp.where((lane & (JP - 1)) == jl, value, weight)

    weight = lax.fori_loop(0, JL, add_weight, jnp.zeros((1, 128), F32))

    pair = jnp.broadcast_to(pair_ref[...].astype(F32), (128, 160)).astype(BF16)
    repeat = one_hot((iota((640, 160), 0) >> 2) == iota((640, 160), 1))
    pair_col = dot_nt(repeat, pair)
    i = iota((640, 128), 0)
    wave = jnp.where((i & 2) == 0, pair_col, (NM - 1.0) - pair_col)
    target = 2.0 * wave + (i & 1).astype(F32)
    to_slots = jnp.concatenate(
        [one_hot(target == (iota((640, 128), 1) + 128 * b).astype(F32)) for b in range(5)],
        axis=1,
    )

    get_grid.wait()
    load_grid(grid_v, spread)
    values = joined(spread).astype(BF16)
    get_table.wait()
    fourier = (dot_nt(table_v[...], values) * weight).astype(BF16)
    slotted = dot(to_slots, fourier)
    for d in range(W):
        send_buf[d] = slotted[40 * d : 40 * d + 40].astype(BF16)

    wait_axis(W)
    exchange_wave(send_buf, recv_buf, send_sem, recv_sem)
    selector = lat_selector(lat_ref)
    wait_bytes(recv_buf, W - 1, recv_sem)
    for g in range(4):
        pieces = rows_to_lanes([recv_buf[4 * g + s].astype(F32) for s in range(4)])
        for r in range(ROWS):
            mixed[g, pl.ds(r, 40, stride=ROWS), :] = pieces[r]
    out_ref[...] = dot_nt(joined(mixed).astype(BF16), selector).astype(BF16)
    wait_bytes(send_buf, W - 1, send_sem)


def exchange_lev(send_buf, recv_buf, send_sem, recv_sem, limit):
    me = lax.axis_index("lev")

    def send(i, carry):
        to = lax.rem(me + i, LV)

        @pl.when(to < limit)
        def _():
            pltpu.make_async_remote_copy(
                src_ref=send_buf.at[to],
                dst_ref=recv_buf.at[me],
                send_sem=send_sem,
                recv_sem=recv_sem,
                device_id={"lev": to},
                device_id_type=MESH,
            ).start()

        return carry

    lax.fori_loop(1, LV, send, 0)


def kernel_b(
    pair_s, slots_ref, stiff_ref, in_ref, modes_in_ref, modes_out_ref, basis_hbm, out_ref,
    basis, out_buf, in_buf, back_buf, home_buf, rows_f, copy_sem, send_sem, recv_sem,
):
    w = lax.axis_index("wave")
    me = lax.axis_index("lev")
    works = me < NB
    signal_axis("lev", LV)
    gets = [
        pltpu.make_async_copy(basis_hbm.at[k], basis.at[k], copy_sem.at[k]) for k in range(SLOTS)
    ]
    for get in gets:
        get.start()

    slots = slots_ref[...]
    picks = [
        one_hot((iota((LEVELS, 256), 0) + LEVELS * f) == slots) for f in range(2)
    ]
    modes_in = jnp.concatenate([dot(modes_in_ref[...], pick) for pick in picks], axis=0)
    modes_in = modes_in.astype(BF16)
    modes_out_t = jnp.transpose(modes_out_ref[...].astype(F32)).astype(BF16)
    modes_out = jnp.concatenate([dot(modes_out_t, pick) for pick in picks], axis=0)
    modes_out = jnp.transpose(modes_out).astype(BF16)
    stiffness = jnp.transpose(jnp.broadcast_to(stiff_ref[...], (128, 128)))
    own = lax.min(me, NB - 1)
    own_pair = pair_s[w * SLOTS + own // 6]
    column = iota((1, 128), 1) + (own % 3) * 128
    degree = jnp.where(column < NM - own_pair, own_pair + column, column - 1).astype(F32)
    growth = degree * (degree + 1.0) / (NM * NM)
    factor = 1.0 / (1.0 + growth * stiffness)

    all_columns = iota((8, COLS), 1)
    for k in range(SLOTS):
        gets[k].wait()
        both = dot(in_ref[16 * k : 16 * k + 16], basis[k])
        first = all_columns < NM - pair_s[w * SLOTS + k]
        picked = jnp.where(first, both[0:8], both[8:16])
        for q in range(2):
            for c in range(3):
                out_buf[6 * k + 3 * q + c] = picked[
                    4 * q : 4 * q + 4, 128 * c : 128 * c + 128
                ].astype(BF16)

    wait_axis(LV)
    exchange_lev(out_buf, in_buf, send_sem.at[0], recv_sem.at[0], NB)

    @pl.when(works)
    def _():
        in_buf[me] = out_buf[me]
        wait_bytes(in_buf, LV - 1, recv_sem.at[0])
        for s in range(LV):
            rows_f[4 * s : 4 * s + 4] = in_buf[s].astype(F32)
        modal = dot(modes_in, rows_f[...].astype(BF16))
        modal = jnp.concatenate([modal[:128] * factor, modal[128:] * factor], axis=0)
        rows_f[...] = dot(modes_out, modal.astype(BF16))
        for s in range(LV):
            back_buf[s] = rows_f[4 * s : 4 * s + 4].astype(BF16)
        exchange_lev(back_buf, home_buf, send_sem.at[1], recv_sem.at[1], LV)
        home_buf[me] = back_buf[me]
        wait_bytes(home_buf, NB - 1, recv_sem.at[1])
        wait_bytes(out_buf, NB - 1, send_sem.at[0])
        wait_bytes(back_buf, LV - 1, send_sem.at[1])

    @pl.when(jnp.logical_not(works))
    def _():
        wait_bytes(home_buf, NB, recv_sem.at[1])
        wait_bytes(out_buf, NB, send_sem.at[0])

    for k in range(SLOTS):
        for q in range(2):
            for c in range(3):
                out_ref[8 * k + 4 * q : 8 * k + 4 * q + 4, 128 * c : 128 * c + 128] = home_buf[
                    6 * k + 3 * q + c
                ].astype(F32)


def kernel_c(
    pair_s, lat_ref, pair_ref, in_ref, basis_hbm, grid_hbm, table_hbm, out_ref,
    basis, grid_v, table_v, spread, back, mixed, send_buf, recv_buf, slotted, copy_sem, send_sem,
    recv_sem,
):
    w = lax.axis_index("wave")
    signal_axis("wave", W)
    gets = [
        pltpu.make_async_copy(basis_hbm.at[k], basis.at[k], copy_sem.at[k]) for k in range(SLOTS)
    ]
    for get in gets:
        get.start()
    get_grid = pltpu.make_async_copy(grid_hbm, grid_v, copy_sem.at[SLOTS])
    get_table = pltpu.make_async_copy(table_hbm, table_v, copy_sem.at[SLOTS + 1])
    get_grid.start()
    get_table.start()

    all_columns = iota((8, COLS), 1)
    for k in range(SLOTS):
        values = in_ref[8 * k : 8 * k + 8]
        first = all_columns < NM - pair_s[w * SLOTS + k]
        both = jnp.concatenate(
            [jnp.where(first, values, 0.0), jnp.where(first, 0.0, values)], axis=0
        ).astype(BF16)
        gets[k].wait()
        back[16 * k : 16 * k + 16] = dot_nt(both, basis[k]).astype(BF16)
    there = dot(back[...], lat_selector(lat_ref))
    for g in range(4):
        mixed[g] = there[:, 128 * g : 128 * g + 128]
    for g in range(4):
        pieces = rows_to_lanes(
            [mixed[g, pl.ds(r, 40, stride=ROWS), :] for r in range(ROWS)]
        )
        for s in range(4):
            send_buf[4 * g + s] = pieces[s].astype(BF16)
    wait_axis(W)
    exchange_wave(send_buf, recv_buf, send_sem, recv_sem)

    pair = jnp.broadcast_to(pair_ref[...].astype(F32), (8, 160)).astype(BF16)
    repeat = one_hot(iota((160, 640), 0) == (iota((160, 640), 1) >> 2))
    pair_row = dot(pair, repeat)[0:1]
    i = iota((1, 640), 1)
    wave = jnp.where((i & 2) == 0, pair_row, (NM - 1.0) - pair_row)
    target = 2.0 * wave + (i & 1).astype(F32)
    from_slots = one_hot(iota((640, 640), 0).astype(F32) == target)
    get_grid.wait()
    load_grid(grid_v, spread)
    get_table.wait()

    wait_bytes(recv_buf, W - 1, recv_sem)
    for d in range(W):
        slotted[40 * d : 40 * d + 40] = recv_buf[d].astype(F32)
    natural = dot(from_slots, slotted[...].astype(BF16))
    fields = dot(jnp.transpose(natural).astype(BF16), table_v[...])
    for b in range(8):
        spread[b] = spread[b] * fields[:, 128 * b : 128 * b + 128]
    for jl in range(JL):
        for b in range(8):
            rows = spread[b, pl.ds(jl, ROWS, stride=JP), :]
            out_ref[jl, :, 128 * b : 128 * b + 128] = rows.astype(BF16)
    wait_bytes(send_buf, W - 1, send_sem)


def params(collective_id):
    return pltpu.CompilerParams(
        collective_id=collective_id, has_side_effects=True, vmem_limit_bytes=60 << 20
    )


def local(
    grid_values,
    legendre,
    gauss_weights,
    modes_in,
    modes_out,
    stiffness,
    slot_pair,
    lat_order,
    field_slots,
):
    table = jnp.asarray(fourier_rows())
    grid = jnp.transpose(grid_values, (1, 0, 2))
    lat_row = lat_order.reshape(1, LAT)
    pair_row = slot_pair.reshape(1, 160)
    grouped = pl.pallas_call(
        kernel_a,
        out_shape=jax.ShapeDtypeStruct((160, LAT), BF16),
        in_specs=[SMEM, SMEM, VMEM, VMEM, HBM, HBM],
        out_specs=VMEM,
        scratch_shapes=[
            pltpu.VMEM((JL, ROWS, NLON), BF16),
            pltpu.VMEM((640, NLON), BF16),
            pltpu.VMEM((8, 128, 128), F32),
            pltpu.VMEM((W, 40, 128), BF16),
            pltpu.VMEM((W, 40, 128), BF16),
            pltpu.VMEM((4, 160, 128), F32),
            DMA((2,)),
            DMA,
            DMA,
        ],
        compiler_params=params(0),
        name="to_spectral",
    )(lat_order, gauss_weights, lat_row, pair_row, grid, table)
    solved = pl.pallas_call(
        kernel_b,
        out_shape=jax.ShapeDtypeStruct((8 * SLOTS, COLS), F32),
        in_specs=[SMEM, VMEM, VMEM, VMEM, VMEM, VMEM, HBM],
        out_specs=VMEM,
        scratch_shapes=[
            pltpu.VMEM((SLOTS, LAT, COLS), BF16),
            pltpu.VMEM((NB, ROWS, 128), BF16),
            pltpu.VMEM((LV, ROWS, 128), BF16),
            pltpu.VMEM((LV, ROWS, 128), BF16),
            pltpu.VMEM((NB, ROWS, 128), BF16),
            pltpu.VMEM((256, 128), F32),
            DMA((SLOTS,)),
            DMA((2,)),
            DMA((2,)),
        ],
        compiler_params=params(1),
        name="vertical",
    )(
        slot_pair,
        field_slots.reshape(1, 256),
        stiffness.reshape(1, 128),
        grouped,
        modes_in,
        modes_out,
        legendre,
    )
    product = pl.pallas_call(
        kernel_c,
        out_shape=jax.ShapeDtypeStruct((JL, ROWS, NLON), BF16),
        in_specs=[SMEM, VMEM, VMEM, VMEM, HBM, HBM, HBM],
        out_specs=VMEM,
        scratch_shapes=[
            pltpu.VMEM((SLOTS, LAT, COLS), BF16),
            pltpu.VMEM((JL, ROWS, NLON), BF16),
            pltpu.VMEM((640, NLON), BF16),
            pltpu.VMEM((8, 128, 128), F32),
            pltpu.VMEM((160, LAT), BF16),
            pltpu.VMEM((4, 160, 128), F32),
            pltpu.VMEM((W, 40, 128), BF16),
            pltpu.VMEM((W, 40, 128), BF16),
            pltpu.VMEM((640, 128), F32),
            DMA((SLOTS + 2,)),
            DMA,
            DMA,
        ],
        compiler_params=params(2),
        name="to_grid",
    )(slot_pair, lat_row, pair_row, solved, legendre, grid, table)
    return jnp.transpose(product, (1, 0, 2))


def solution(mesh):
    in_specs = (P("lev", "wave", None), P("wave", None, None), P(), P(), P(), P(), P(), P(), P())
    out_specs = P("lev", "wave", None)
    return jax.shard_map(local, mesh=mesh, in_specs=in_specs, out_specs=out_specs, check_vma=False)
```

time: 141 us -> 71.4 us (0.51)
  Pallas kernels: 0 us -> 69.3 us
  local copies, waits for them, and re-layouts: 40.5 us -> 1.72 us
  starting transfers between devices: 36 us -> 0 us
  waiting for transfers between devices: 24.2 us -> 0 us
  blocking collectives: 17.1 us -> 0 us
  other arithmetic: 14.4 us -> 0 us
  matrix products: 7.32 us -> 0 us
    pallas_call x0 -> x3, Pallas kernels: none -> 69.3 us  [the longest x1 27.5 us: local(): pl.pallas_call(kernel_b, out_shape=jax.ShapeDtypeStruct((8 * SLOTS, COLS)...]
    all_to_all x3 -> x0, starting transfers between devices: 36 us -> none  [the longest x1 18.2 us: local(): lax.all_to_all(fourier, 'wave', split_axis=2, concat_axis=1, tiled=True)]
    all_to_all x3 -> x0, waiting for transfers between devices: 24.2 us -> none  [the longest x1 11.1 us: local(): lax.all_to_all(flattened, 'lev', split_axis=1, concat_axis=0, tiled=True)]
    all_to_all x1 -> x0, blocking collectives: 17.1 us -> none  [local(): lax.all_to_all(back_rows, 'wave', split_axis=1, concat_axis=2, tiled=True)]
    scatter x3 -> x0, local copies, waits for them, and re-layouts: 16.4 us -> none  [the longest x2 15.2 us: local(): true_order = jnp.zeros_like(arrived).at[:, lat_order].set(arrived)]
    gather x5 -> x0, local copies, waits for them, and re-layouts: 9.88 us -> none  [the longest x2 7.01 us: local(): fourier_back[:, lat_order].reshape(block_rows, lat_count, slot_local * 4)]
    dot_general x5 -> x0, matrix products: 7.32 us -> none  [the longest x1 3.32 us: local(): jnp.einsum('afkrc,kjc->fjkar', split_waves, legendre, preferred_element_t...]
    div x2 -> x0, other arithmetic: 6.34 us -> none  [the longest x1 6.25 us: local(): growth = degree * (degree + 1.0) / (NM * NM)]
  transfers between devices with their start and end apart: 3 -> 0, of which waited for: 3 -> 0; matrix products, arithmetic and copies ran while one was open for 5% -> 0% of each run, Pallas kernels for 0% -> 0%
where the time goes in v1:
time: 71.4 us; the launch traced here: 71.1 us
  Pallas kernels  69.3 us (97%)
  local copies, waits for them, and re-layouts  1.72 us (2%)
    pallas_call x1, Pallas kernels, local(): pl.pallas_call(kernel_b, out_shape=jax.ShapeDtypeStruct((8 * SLOTS, COLS)...  27.5 us
    pallas_call x1, Pallas kernels, local(): pl.pallas_call(kernel_a, out_shape=jax.ShapeDtypeStruct((160, LAT), BF16)...  25.7 us
    pallas_call x1, Pallas kernels, local(): pl.pallas_call(kernel_c, out_shape=jax.ShapeDtypeStruct((JL, ROWS, NLON),...  16.1 us
    unnamed x1, local copies, waits for them, and re-layouts  1.72 us

profile of v1, /device:TPU:1, one launch (start us, length us, event | category | flops | bytes accessed | tf_op | source)
XLA Modules:
  0.0 71.1 jit_solution(16735604536739695422)
XLA Ops:
  0.0 25.7 %to_spectral.1.in_ref = bf16[160,480]{1,0:T(8,128)(2,1)} custom-call(s32[480]{0:T(512)} %lat_s.1, f32[480]{0:T(512)} %gauss_s.1, s32[1,480]{1,0:T(1,128)} %bitcast.9, s32[1,160]{1,0:T(1,128)} %bitcast.11, bf16[30,4,1024]{2,1,0:T(4,128)(2,1)} %bitcast.6, bf16[640,1024]{1,0:T(8,128)(2,1)} %constant.2.clone.table_hbm), custom_call_target="tpu_custom_call" | custom-call | tf_op jit(solution)/shard_map/to_spectral/pallas_call | solution.py:361
  25.7 27.5 %vertical.1.in_ref = f32[80,384]{1,0:T(8,128)} custom-call(s32[160]{0:T(256)} %pair_s.3, s32[1,256]{1,0:T(1,128)} %bitcast.13, f32[1,128]{1,0:T(1,128)} %bitcast.14, bf16[160,480]{1,0:T(8,128)(2,1)} %to_spectral.1.in_ref, bf16[128,128]{1,0:T(8,128)(2,1)} %modes_in_ref.1, bf16[128,128]{1,0:T(8,128)(2,1)} %modes_out_ref.1, bf16[10,480,384]{2,1,0:T(8,128)(2,1)} %basis_hbm.3), custom_call_target="tpu_custom_call" | custom-call | tf_op jit(solution)/shard_map/vertical/pallas_call | solution.py:380
  53.3 16.1 %to_grid.1 = bf16[30,4,1024]{2,1,0:T(4,128)(2,1)} custom-call(s32[160]{0:T(256)} %pair_s.3, s32[1,480]{1,0:T(1,128)} %bitcast.10, s32[1,160]{1,0:T(1,128)} %bitcast.12, f32[80,384]{1,0:T(8,128)} %vertical.1.in_ref, bf16[10,480,384]{2,1,0:T(8,128)(2,1)} %basis_hbm.3, bf16[30,4,1024]{2,1,0:T(4,128)(2,1)} %bitcast.7, bf16[640,1024]{1,0:T(8,128)(2,1)} %constant.2.clone.table_hbm), custom_call_target="tpu_custom_call" | custom-call | tf_op jit(solution)/shard_map/to_grid/pallas_call | solution.py:407
  69.3 1.7 %copy.12 = bf16[4,30,1024]{2,0,1:T(4,128)(2,1)} copy(bf16[4,30,1024]{2,0,1:T(4,128)(2,1)} %bitcast.8) | data formatting | bytes 491520

commit v2 on v0

v2 whole, which is shorter than its diff:
```python
import functools

import jax
import jax.numpy as jnp
import numpy as np
from jax import lax
from jax.experimental import pallas as pl
from jax.experimental.pallas import tpu as pltpu
from jax.sharding import PartitionSpec as P

NM = 320
LEVELS = 128
W = 16
LV = 64
ROWS = 4
JL = 30
JP = 32
SLOTS = 10
LAT = 480
COLS = 384
NB = 60
NLON = 1024
F32 = jnp.float32
BF16 = jnp.bfloat16
MESH = pl.DeviceIdType.MESH
HBM = pl.BlockSpec(memory_space=pltpu.HBM)
VMEM = pltpu.VMEM
SMEM = pltpu.SMEM
DMA = pltpu.SemaphoreType.DMA


def fourier_rows():
    steps = (np.arange(NM)[:, None] * np.arange(NLON)[None, :]) % NLON
    angles = steps.astype(np.float32) * np.float32(2.0 * np.pi / NLON)
    entries = np.stack([np.cos(angles), -np.sin(angles)], axis=1) / np.float32(32.0)
    return entries.reshape(2 * NM, NLON).astype(jnp.bfloat16)


def iota(shape, axis):
    return lax.broadcasted_iota(jnp.int32, shape, axis)


def one_hot(condition):
    return jnp.where(condition, 1.0, 0.0).astype(F32).astype(BF16)


def dot(a, b):
    return jnp.dot(a, b, preferred_element_type=F32)


def dot_nt(a, b):
    return lax.dot_general(a, b, (((1,), (1,)), ((), ())), preferred_element_type=F32)


def far_first(step):
    half = (step + 1) // 2
    return 4 + jnp.where(step % 2 == 0, half, -half)


def wave_partner(step):
    w = lax.axis_index("wave")
    z = (w // 2 + far_first(step // 2)) % 8
    return z * 2 + (w % 2 + 1 - step % 2) % 2


def lev_partner(step):
    me = lax.axis_index("lev")
    x = (me // 8 + far_first(step // 8)) % 8
    y = (me % 8 + far_first(step % 8)) % 8
    return x * 8 + y


def each(count, body):
    def step(i, carry):
        body(i)
        return carry

    lax.fori_loop(0, count, step, 0, unroll=True)


def enter():
    barrier = pltpu.get_barrier_semaphore()

    def greet_lev(i):
        pl.semaphore_signal(
            barrier, inc=1, device_id={"lev": lev_partner(i)}, device_id_type=MESH
        )

    def greet_wave(i):
        pl.semaphore_signal(
            barrier, inc=1, device_id={"wave": wave_partner(i)}, device_id_type=MESH
        )

    each(LV - 1, greet_lev)
    each(W - 1, greet_wave)


def wait_bytes(ref, count, sem):
    part = ref.at[pl.ds(0, count)]
    pltpu.make_async_copy(part, part, sem).wait()


def lat_selector(lat):
    j = iota((LAT, W * JP), 0)
    jp = iota((LAT, W * JP), 1)
    local = jp & (JP - 1)
    spread = one_hot((j == (jp >> 5) * JL + local) & (local < JL))
    high = jnp.broadcast_to((lat >> 5).astype(F32), (8, LAT)).astype(BF16)
    low = jnp.broadcast_to((lat & 31).astype(F32), (8, LAT)).astype(BF16)
    there = dot(high, spread)[0:1] * 32.0 + dot(low, spread)[0:1]
    there = jnp.where((iota((1, W * JP), 1) & (JP - 1)) < JL, there, -1.0)
    return one_hot(iota((LAT, W * JP), 0).astype(F32) == there)


def table_rows(pair, index):
    wave = jnp.where((index & 2) == 0, pair, (NM - 1.0) - pair)
    return 2.0 * wave + (index & 1).astype(F32)


def to_slots(pair):
    pair = jnp.broadcast_to(pair.astype(F32), (128, 160)).astype(BF16)
    repeat = one_hot((iota((640, 160), 0) >> 2) == iota((640, 160), 1))
    target = table_rows(dot_nt(repeat, pair), iota((640, 128), 0))
    blocks = [
        one_hot(target == (iota((640, 128), 1) + 128 * b).astype(F32)) for b in range(5)
    ]
    return jnp.concatenate(blocks, axis=1)


def from_slots(pair):
    pair = jnp.broadcast_to(pair.astype(F32), (8, 160)).astype(BF16)
    repeat = one_hot(iota((160, 640), 0) == (iota((160, 640), 1) >> 2))
    target = table_rows(dot(pair, repeat)[0:1], iota((1, 640), 1))
    return one_hot(iota((640, 640), 0).astype(F32) == target)


def rows_to_lanes(pieces):
    return [
        jnp.concatenate([piece[:, JP * b : JP * b + JP] for piece in pieces], axis=1)
        for b in range(4)
    ]


def joined(ref):
    return jnp.concatenate([ref[b] for b in range(ref.shape[0])], axis=1)


def send_wave(send_buf, recv_buf, send_sem, recv_sem):
    w = lax.axis_index("wave")

    def send(i):
        to = wave_partner(i)
        pltpu.make_async_remote_copy(
            src_ref=send_buf.at[to],
            dst_ref=recv_buf.at[w],
            send_sem=send_sem,
            recv_sem=recv_sem,
            device_id={"wave": to},
            device_id_type=MESH,
        ).start()

    each(W - 1, send)
    recv_buf[w] = send_buf[w]


def send_lev(send_buf, recv_buf, send_sem, recv_sem, limit):
    me = lax.axis_index("lev")

    def send(i):
        to = lev_partner(i)

        def start():
            pltpu.make_async_remote_copy(
                src_ref=send_buf.at[to],
                dst_ref=recv_buf.at[me],
                send_sem=send_sem,
                recv_sem=recv_sem,
                device_id={"lev": to},
                device_id_type=MESH,
            ).start()

        if limit == LV:
            start()
        else:
            pl.when(to < limit)(start)

    each(LV - 1, send)


def kernel(
    lat_hbm, gauss_hbm, pair_hbm, lat_row, pair_row, slots_row, stiff_row, modes_in_hbm,
    modes_out_hbm, grid_hbm, table_hbm, basis_hbm, out_ref,
    lat_s, gauss_s, pair_s, lat_v, pair_v, slots_v, stiff_v, modes_in_v, modes_out_v, grid_v,
    table_v, basis, spread, send_a, recv_a, mixed, degrees, selector, slot_rows, modes_a,
    modes_b, factor_v, out_b, in_b, back_b, home_b, rows_f, send_c, recv_c, slotted,
    copy_sem, send_sem, recv_sem,
):
    w = lax.axis_index("wave")
    me = lax.axis_index("lev")
    works = me < NB
    enter()
    pairs = [
        (grid_hbm, grid_v), (pair_row, pair_v), (lat_hbm, lat_s), (gauss_hbm, gauss_s),
        (table_hbm, table_v), (pair_hbm, pair_s), (lat_row, lat_v), (slots_row, slots_v),
        (stiff_row, stiff_v), (modes_in_hbm, modes_in_v), (modes_out_hbm, modes_out_v),
        (basis_hbm, basis),
    ]
    gets = [pltpu.make_async_copy(a, b, copy_sem.at[i]) for i, (a, b) in enumerate(pairs)]
    for get in gets:
        get.start()

    gets[1].wait()
    slot_order = to_slots(pair_v[...])
    spread[...] = jnp.zeros_like(spread)
    gets[0].wait()
    for jl in range(JL):
        rows = grid_v[jl].astype(F32)
        for b in range(8):
            spread[b, pl.ds(jl, ROWS, stride=JP), :] = rows[:, 128 * b : 128 * b + 128]
    values = joined(spread).astype(BF16)
    gets[2].wait()
    gets[3].wait()
    lane = iota((1, 128), 1)

    def add_weight(jl, weight):
        value = gauss_s[lat_s[w * JL + jl]]
        return jnp.where((lane & (JP - 1)) == jl, value, weight)

    weight = lax.fori_loop(0, JL, add_weight, jnp.zeros((1, 128), F32), unroll=True)
    gets[4].wait()
    fourier = (dot_nt(table_v[...], values) * weight).astype(BF16)
    slots = dot(slot_order, fourier)
    for d in range(W):
        send_a[d] = slots[40 * d : 40 * d + 40].astype(BF16)
    pl.semaphore_wait(pltpu.get_barrier_semaphore(), LV + W - 2)
    send_wave(send_a, recv_a, send_sem.at[0], recv_sem.at[0])

    for get in gets[5:11]:
        get.wait()
    selector[...] = lat_selector(lat_v[...])
    picks = [
        one_hot((iota((LEVELS, 256), 0) + LEVELS * f) == slots_v[...]) for f in range(2)
    ]
    modes = jnp.concatenate([dot(modes_in_v[...], pick) for pick in picks], axis=0)
    modes_a[...] = modes.astype(BF16)
    modes_t = jnp.transpose(modes_out_v[...].astype(F32)).astype(BF16)
    modes = jnp.concatenate([dot(modes_t, pick) for pick in picks], axis=0)
    modes_b[...] = jnp.transpose(modes).astype(BF16)
    stiffness = jnp.transpose(jnp.broadcast_to(stiff_v[...], (128, 128)))
    own_pair = pair_s[w * SLOTS + lax.min(me, NB - 1) // 6]
    column = lane + (me % 3) * 128
    degree = jnp.where(column < NM - own_pair, own_pair + column, column - 1).astype(F32)
    growth = degree * (degree + 1.0) / (NM * NM)
    factor_v[...] = 1.0 / (1.0 + growth * stiffness)
    slot_rows[...] = from_slots(pair_v[...])
    gets[11].wait()

    wait_bytes(recv_a, W - 1, recv_sem.at[0])
    for g in range(4):
        pieces = rows_to_lanes([recv_a[4 * g + s].astype(F32) for s in range(4)])
        for r in range(ROWS):
            mixed[g, pl.ds(r, 40, stride=ROWS), :] = pieces[r]
    degrees[...] = dot_nt(joined(mixed).astype(BF16), selector[...]).astype(BF16)
    all_columns = iota((8, COLS), 1)
    firsts = [all_columns < NM - pair_s[w * SLOTS + k] for k in range(SLOTS)]
    for k in range(SLOTS):
        both = dot(degrees[16 * k : 16 * k + 16], basis[k])
        picked = jnp.where(firsts[k], both[0:8], both[8:16])
        for q in range(2):
            for c in range(3):
                out_b[6 * k + 3 * q + c] = picked[
                    4 * q : 4 * q + 4, 128 * c : 128 * c + 128
                ].astype(BF16)
    send_lev(out_b, in_b, send_sem.at[1], recv_sem.at[1], NB)

    @pl.when(works)
    def _():
        in_b[me] = out_b[me]
        wait_bytes(in_b, LV - 1, recv_sem.at[1])
        for s in range(LV):
            rows_f[4 * s : 4 * s + 4] = in_b[s].astype(F32)
        modal = dot(modes_a[...], rows_f[...].astype(BF16))
        factor = factor_v[...]
        modal = jnp.concatenate([modal[:128] * factor, modal[128:] * factor], axis=0)
        rows_f[...] = dot(modes_b[...], modal.astype(BF16))
        for s in range(LV):
            back_b[s] = rows_f[4 * s : 4 * s + 4].astype(BF16)
        send_lev(back_b, home_b, send_sem.at[2], recv_sem.at[2], LV)
        home_b[me] = back_b[me]
        wait_bytes(home_b, NB - 1, recv_sem.at[2])

    @pl.when(jnp.logical_not(works))
    def _():
        wait_bytes(home_b, NB, recv_sem.at[2])

    for k in range(SLOTS):
        values = jnp.concatenate(
            [
                jnp.concatenate(
                    [home_b[6 * k + 3 * q + c].astype(F32) for c in range(3)], axis=1
                )
                for q in range(2)
            ],
            axis=0,
        )
        both = jnp.concatenate(
            [jnp.where(firsts[k], values, 0.0), jnp.where(firsts[k], 0.0, values)], axis=0
        )
        degrees[16 * k : 16 * k + 16] = dot_nt(both.astype(BF16), basis[k]).astype(BF16)
    there = dot(degrees[...], selector[...])
    for g in range(4):
        mixed[g] = there[:, 128 * g : 128 * g + 128]
    for g in range(4):
        pieces = rows_to_lanes(
            [mixed[g, pl.ds(r, 40, stride=ROWS), :] for r in range(ROWS)]
        )
        for s in range(4):
            send_c[4 * g + s] = pieces[s].astype(BF16)
    send_wave(send_c, recv_c, send_sem.at[3], recv_sem.at[3])

    @pl.when(works)
    def _():
        wait_bytes(out_b, NB - 1, send_sem.at[1])
        wait_bytes(back_b, LV - 1, send_sem.at[2])

    @pl.when(jnp.logical_not(works))
    def _():
        wait_bytes(out_b, NB, send_sem.at[1])

    wait_bytes(send_a, W - 1, send_sem.at[0])

    wait_bytes(recv_c, W - 1, recv_sem.at[3])
    for d in range(W):
        slotted[40 * d : 40 * d + 40] = recv_c[d].astype(F32)
    natural = dot(slot_rows[...], slotted[...].astype(BF16))
    fields = dot(jnp.transpose(natural).astype(BF16), table_v[...])
    for b in range(8):
        spread[b] = spread[b] * fields[:, 128 * b : 128 * b + 128]
    for jl in range(JL):
        for b in range(8):
            rows = spread[b, pl.ds(jl, ROWS, stride=JP), :]
            out_ref[jl, :, 128 * b : 128 * b + 128] = rows.astype(BF16)
    wait_bytes(send_c, W - 1, send_sem.at[3])


def local(
    grid_values,
    legendre,
    gauss_weights,
    modes_in,
    modes_out,
    stiffness,
    slot_pair,
    lat_order,
    field_slots,
):
    product = pl.pallas_call(
        kernel,
        out_shape=jax.ShapeDtypeStruct((JL, ROWS, NLON), BF16),
        in_specs=[HBM] * 12,
        out_specs=pl.BlockSpec(memory_space=VMEM),
        scratch_shapes=[
            SMEM((LAT,), jnp.int32),
            SMEM((LAT,), F32),
            SMEM((160,), jnp.int32),
            VMEM((1, LAT), jnp.int32),
            VMEM((1, 160), jnp.int32),
            VMEM((1, 256), jnp.int32),
            VMEM((1, 128), F32),
            VMEM((LEVELS, LEVELS), BF16),
            VMEM((LEVELS, LEVELS), BF16),
            VMEM((JL, ROWS, NLON), BF16),
            VMEM((640, NLON), BF16),
            VMEM((SLOTS, LAT, COLS), BF16),
            VMEM((8, 128, 128), F32),
            VMEM((W, 40, 128), BF16),
            VMEM((W, 40, 128), BF16),
            VMEM((4, 160, 128), F32),
            VMEM((160, LAT), BF16),
            VMEM((LAT, W * JP), BF16),
            VMEM((640, 640), BF16),
            VMEM((256, 256), BF16),
            VMEM((256, 256), BF16),
            VMEM((LEVELS, 128), F32),
            VMEM((NB, ROWS, 128), BF16),
            VMEM((LV, ROWS, 128), BF16),
            VMEM((LV, ROWS, 128), BF16),
            VMEM((NB, ROWS, 128), BF16),
            VMEM((256, 128), F32),
            VMEM((W, 40, 128), BF16),
            VMEM((W, 40, 128), BF16),
            VMEM((640, 128), F32),
            DMA((12,)),
            DMA((4,)),
            DMA((4,)),
        ],
        compiler_params=pltpu.CompilerParams(
            collective_id=0, has_side_effects=True, vmem_limit_bytes=60 << 20
        ),
        name="transform_step",
    )(
        lat_order,
        gauss_weights,
        slot_pair,
        lat_order.reshape(1, LAT),
        slot_pair.reshape(1, 160),
        field_slots.reshape(1, 256),
        stiffness.reshape(1, 128),
        modes_in,
        modes_out,
        jnp.transpose(grid_values, (1, 0, 2)),
        jnp.asarray(fourier_rows()),
        legendre,
    )
    return jnp.transpose(product, (1, 0, 2))


def solution(mesh):
    in_specs = (P("lev", "wave", None), P("wave", None, None), P(), P(), P(), P(), P(), P(), P())
    out_specs = P("lev", "wave", None)
    return jax.shard_map(local, mesh=mesh, in_specs=in_specs, out_specs=out_specs, check_vma=False)
```

time: 141 us -> 56.1 us (0.40)
  Pallas kernels: 0 us -> 54.2 us
  local copies, waits for them, and re-layouts: 40.5 us -> 1.72 us
  starting transfers between devices: 36 us -> 0 us
  waiting for transfers between devices: 24.2 us -> 0 us
  blocking collectives: 17.1 us -> 0 us
  other arithmetic: 14.4 us -> 0 us
  matrix products: 7.32 us -> 0 us
    pallas_call x0 -> x1, Pallas kernels: none -> 54.2 us  [local(): pl.pallas_call(kernel, out_shape=jax.ShapeDtypeStruct((JL, ROWS, NLON), B...]
    all_to_all x3 -> x0, starting transfers between devices: 36 us -> none  [the longest x1 18.2 us: local(): lax.all_to_all(fourier, 'wave', split_axis=2, concat_axis=1, tiled=True)]
    all_to_all x3 -> x0, waiting for transfers between devices: 24.2 us -> none  [the longest x1 11.1 us: local(): lax.all_to_all(flattened, 'lev', split_axis=1, concat_axis=0, tiled=True)]
    all_to_all x1 -> x0, blocking collectives: 17.1 us -> none  [local(): lax.all_to_all(back_rows, 'wave', split_axis=1, concat_axis=2, tiled=True)]
    scatter x3 -> x0, local copies, waits for them, and re-layouts: 16.4 us -> none  [the longest x2 15.2 us: local(): true_order = jnp.zeros_like(arrived).at[:, lat_order].set(arrived)]
    gather x5 -> x0, local copies, waits for them, and re-layouts: 9.88 us -> none  [the longest x2 7.01 us: local(): fourier_back[:, lat_order].reshape(block_rows, lat_count, slot_local * 4)]
    dot_general x5 -> x0, matrix products: 7.32 us -> none  [the longest x1 3.32 us: local(): jnp.einsum('afkrc,kjc->fjkar', split_waves, legendre, preferred_element_t...]
    div x2 -> x0, other arithmetic: 6.34 us -> none  [the longest x1 6.25 us: local(): growth = degree * (degree + 1.0) / (NM * NM)]
  transfers between devices with their start and end apart: 3 -> 0, of which waited for: 3 -> 0; matrix products, arithmetic and copies ran while one was open for 5% -> 0% of each run, Pallas kernels for 0% -> 0%
where the time goes in v2:
time: 56.1 us; the launch traced here: 55.9 us
  Pallas kernels  54.2 us (97%)
  local copies, waits for them, and re-layouts  1.72 us (3%)
    pallas_call x1, Pallas kernels, local(): pl.pallas_call(kernel, out_shape=jax.ShapeDtypeStruct((JL, ROWS, NLON), B...  54.2 us
    unnamed x1, local copies, waits for them, and re-layouts  1.72 us

profile of v2, /device:TPU:1, one launch (start us, length us, event | category | flops | bytes accessed | tf_op | source)
XLA Modules:
  0.0 55.9 jit_solution(15296614097873210124)
XLA Ops:
  0.0 54.2 %transform_step.1 = bf16[30,4,1024]{2,1,0:T(4,128)(2,1)} custom-call(s32[480]{0:T(512)} %lat_hbm.1, f32[480]{0:T(512)} %gauss_hbm.1, s32[160]{0:T(256)} %pair_hbm.1, s32[1,480]{1,0:T(1,128)} %bitcast.8, s32[1,160]{1,0:T(1,128)} %bitcast.9, s32[1,256]{1,0:T(1,128)} %bitcast.10, f32[1,128]{1,0:T(1,128)} %bitcast.11, bf16[128,128]{1,0:T(8,128)(2,1)} %modes_in_hbm.1, ...), custom_call_target="tpu_custom_call" | custom-call | tf_op jit(solution)/shard_map/transform_step/pallas_call | solution.py:357
  54.2 1.7 %copy.12 = bf16[4,30,1024]{2,0,1:T(4,128)(2,1)} copy(bf16[4,30,1024]{2,0,1:T(4,128)(2,1)} %bitcast.6) | data formatting | bytes 491520

commit v3 on v2

--- a/solution.py
+++ b/solution.py
@@ -52,47 +52,61 @@
     return lax.dot_general(a, b, (((1,), (1,)), ((), ())), preferred_element_type=F32)
 
 
-def far_first(step):
-    half = (step + 1) // 2
-    return 4 + jnp.where(step % 2 == 0, half, -half)
-
-
-def wave_partner(step):
+def ring_distance(step):
+    return min(step, 8 - step)
+
+
+WAVE_STEPS = sorted(
+    [(z, core) for z in range(8) for core in range(2) if z or core],
+    key=lambda step: -ring_distance(step[0]),
+)
+LEV_STEPS = sorted(
+    [(x, y) for x in range(8) for y in range(8) if x or y],
+    key=lambda step: -ring_distance(step[0]) - ring_distance(step[1]),
+)
+RING_STEPS = sorted(range(1, 8), key=lambda step: -ring_distance(step))
+
+
+def wave_partners():
     w = lax.axis_index("wave")
-    z = (w // 2 + far_first(step // 2)) % 8
-    return z * 2 + (w % 2 + 1 - step % 2) % 2
-
-
-def lev_partner(step):
+    z, core = lax.div(w, 2), lax.rem(w, 2)
+    chips = [lax.rem(z + step, 8) * 2 for step in range(8)]
+    cores = [core, 1 - core]
+    return [chips[a] + cores[b] for a, b in WAVE_STEPS]
+
+
+def lev_places():
     me = lax.axis_index("lev")
-    x = (me // 8 + far_first(step // 8)) % 8
-    y = (me % 8 + far_first(step % 8)) % 8
-    return x * 8 + y
-
-
-def each(count, body):
-    def step(i, carry):
-        body(i)
-        return carry
-
-    lax.fori_loop(0, count, step, 0, unroll=True)
+    x, y = lax.div(me, 8), lax.rem(me, 8)
+    return (
+        [lax.rem(x + step, 8) * 8 for step in range(8)],
+        [lax.rem(y + step, 8) for step in range(8)],
+    )
+
+
+def lev_partners():
+    xs, ys = lev_places()
+    return [xs[a] + ys[b] for a, b in LEV_STEPS]
+
+
+def signal(semaphore, axis, to):
+    pl.semaphore_signal(semaphore, inc=1, device_id={axis: to}, device_id_type=MESH)
 
 
 def enter():
     barrier = pltpu.get_barrier_semaphore()
-
-    def greet_lev(i):
-        pl.semaphore_signal(
-            barrier, inc=1, device_id={"lev": lev_partner(i)}, device_id_type=MESH
-        )
-
-    def greet_wave(i):
-        pl.semaphore_signal(
-            barrier, inc=1, device_id={"wave": wave_partner(i)}, device_id_type=MESH
-        )
-
-    each(LV - 1, greet_lev)
-    each(W - 1, greet_wave)
+    xs, ys = lev_places()
+    for step in RING_STEPS:
+        signal(barrier, "lev", xs[step] + ys[0])
+        signal(barrier, "lev", xs[0] + ys[step])
+    for to in wave_partners():
+        signal(barrier, "wave", to)
+
+
+def pass_on(semaphore):
+    xs, ys = lev_places()
+    for step in RING_STEPS:
+        signal(semaphore, "lev", xs[0] + ys[step])
 
 
 def wait_bytes(ref, count, sem):
@@ -127,13 +141,6 @@
     return jnp.concatenate(blocks, axis=1)
 
 
-def from_slots(pair):
-    pair = jnp.broadcast_to(pair.astype(F32), (8, 160)).astype(BF16)
-    repeat = one_hot(iota((160, 640), 0) == (iota((160, 640), 1) >> 2))
-    target = table_rows(dot(pair, repeat)[0:1], iota((1, 640), 1))
-    return one_hot(iota((640, 640), 0).astype(F32) == target)
-
-
 def rows_to_lanes(pieces):
     return [
         jnp.concatenate([piece[:, JP * b : JP * b + JP] for piece in pieces], axis=1)
@@ -147,9 +154,7 @@
 
 def send_wave(send_buf, recv_buf, send_sem, recv_sem):
     w = lax.axis_index("wave")
-
-    def send(i):
-        to = wave_partner(i)
+    for to in wave_partners():
         pltpu.make_async_remote_copy(
             src_ref=send_buf.at[to],
             dst_ref=recv_buf.at[w],
@@ -158,47 +163,37 @@
             device_id={"wave": to},
             device_id_type=MESH,
         ).start()
-
-    each(W - 1, send)
     recv_buf[w] = send_buf[w]
 
 
 def send_lev(send_buf, recv_buf, send_sem, recv_sem, limit):
     me = lax.axis_index("lev")
-
-    def send(i):
-        to = lev_partner(i)
-
-        def start():
-            pltpu.make_async_remote_copy(
-                src_ref=send_buf.at[to],
-                dst_ref=recv_buf.at[me],
-                send_sem=send_sem,
-                recv_sem=recv_sem,
-                device_id={"lev": to},
-                device_id_type=MESH,
-            ).start()
-
+    for to in lev_partners():
+        copy = pltpu.make_async_remote_copy(
+            src_ref=send_buf.at[to],
+            dst_ref=recv_buf.at[me],
+            send_sem=send_sem,
+            recv_sem=recv_sem,
+            device_id={"lev": to},
+            device_id_type=MESH,
+        )
         if limit == LV:
-            start()
+            copy.start()
         else:
-            pl.when(to < limit)(start)
-
-    each(LV - 1, send)
+            pl.when(to < limit)(copy.start)
 
 
 def kernel(
     lat_hbm, gauss_hbm, pair_hbm, lat_row, pair_row, slots_row, stiff_row, modes_in_hbm,
     modes_out_hbm, grid_hbm, table_hbm, basis_hbm, out_ref,
     lat_s, gauss_s, pair_s, lat_v, pair_v, slots_v, stiff_v, modes_in_v, modes_out_v, grid_v,
-    table_v, basis, spread, send_a, recv_a, mixed, degrees, selector, slot_rows, modes_a,
+    table_v, basis, spread, send_a, recv_a, mixed, degrees, selector, slot_order, slot_table, modes_a,
     modes_b, factor_v, out_b, in_b, back_b, home_b, rows_f, send_c, recv_c, slotted,
-    copy_sem, send_sem, recv_sem,
+    copy_sem, send_sem, recv_sem, ring_sem,
 ):
     w = lax.axis_index("wave")
     me = lax.axis_index("lev")
     works = me < NB
-    enter()
     pairs = [
         (grid_hbm, grid_v), (pair_row, pair_v), (lat_hbm, lat_s), (gauss_hbm, gauss_s),
         (table_hbm, table_v), (pair_hbm, pair_s), (lat_row, lat_v), (slots_row, slots_v),
@@ -208,9 +203,10 @@
     gets = [pltpu.make_async_copy(a, b, copy_sem.at[i]) for i, (a, b) in enumerate(pairs)]
     for get in gets:
         get.start()
+    enter()
 
     gets[1].wait()
-    slot_order = to_slots(pair_v[...])
+    slot_order[...] = to_slots(pair_v[...])
     spread[...] = jnp.zeros_like(spread)
     gets[0].wait()
     for jl in range(JL):
@@ -229,10 +225,11 @@
     weight = lax.fori_loop(0, JL, add_weight, jnp.zeros((1, 128), F32), unroll=True)
     gets[4].wait()
     fourier = (dot_nt(table_v[...], values) * weight).astype(BF16)
-    slots = dot(slot_order, fourier)
+    slots = dot(slot_order[...], fourier)
     for d in range(W):
         send_a[d] = slots[40 * d : 40 * d + 40].astype(BF16)
-    pl.semaphore_wait(pltpu.get_barrier_semaphore(), LV + W - 2)
+    pl.semaphore_wait(pltpu.get_barrier_semaphore(), W - 1 + 14)
+    pass_on(ring_sem)
     send_wave(send_a, recv_a, send_sem.at[0], recv_sem.at[0])
 
     for get in gets[5:11]:
@@ -252,7 +249,6 @@
     degree = jnp.where(column < NM - own_pair, own_pair + column, column - 1).astype(F32)
     growth = degree * (degree + 1.0) / (NM * NM)
     factor_v[...] = 1.0 / (1.0 + growth * stiffness)
-    slot_rows[...] = from_slots(pair_v[...])
     gets[11].wait()
 
     wait_bytes(recv_a, W - 1, recv_sem.at[0])
@@ -271,7 +267,12 @@
                 out_b[6 * k + 3 * q + c] = picked[
                     4 * q : 4 * q + 4, 128 * c : 128 * c + 128
                 ].astype(BF16)
+    pl.semaphore_wait(ring_sem, 7)
     send_lev(out_b, in_b, send_sem.at[1], recv_sem.at[1], NB)
+
+    for b in range(5):
+        part = pl.ds(128 * b, 128)
+        slot_table[part] = dot(slot_order[part], table_v[...]).astype(BF16)
 
     @pl.when(works)
     def _():
@@ -332,8 +333,7 @@
     wait_bytes(recv_c, W - 1, recv_sem.at[3])
     for d in range(W):
         slotted[40 * d : 40 * d + 40] = recv_c[d].astype(F32)
-    natural = dot(slot_rows[...], slotted[...].astype(BF16))
-    fields = dot(jnp.transpose(natural).astype(BF16), table_v[...])
+    fields = dot(jnp.transpose(slotted[...]).astype(BF16), slot_table[...])
     for b in range(8):
         spread[b] = spread[b] * fields[:, 128 * b : 128 * b + 128]
     for jl in range(JL):
@@ -356,7 +356,7 @@
 ):
     product = pl.pallas_call(
         kernel,
-        out_shape=jax.ShapeDtypeStruct((JL, ROWS, NLON), BF16),
+        out_shape=VMEM((JL, ROWS, NLON), BF16),
         in_specs=[HBM] * 12,
         out_specs=pl.BlockSpec(memory_space=VMEM),
         scratch_shapes=[
@@ -379,6 +379,7 @@
             VMEM((160, LAT), BF16),
             VMEM((LAT, W * JP), BF16),
             VMEM((640, 640), BF16),
+            VMEM((640, NLON), BF16),
             VMEM((256, 256), BF16),
             VMEM((256, 256), BF16),
             VMEM((LEVELS, 128), F32),
@@ -393,6 +394,7 @@
             DMA((12,)),
             DMA((4,)),
             DMA((4,)),
+            pltpu.SemaphoreType.REGULAR,
         ],
         compiler_params=pltpu.CompilerParams(
             collective_id=0, has_side_effects=True, vmem_limit_bytes=60 << 20

time: 56.1 us -> 50.6 us (0.902)
  Pallas kernels: 54.2 us -> 49.7 us
  local copies, waits for them, and re-layouts: 1.72 us -> 0.7 us
    pallas_call x1, Pallas kernels: 54.2 us -> 49.7 us  [local(): pl.pallas_call(kernel, out_shape=VMEM((JL, ROWS, NLON), BF16), in_specs=[...]
    unnamed x1, local copies, waits for them, and re-layouts: 1.72 us -> 0.7 us
where the time goes in v3:
time: 50.6 us; the launch traced here: 50.4 us
  Pallas kernels  49.7 us (98%)
  local copies, waits for them, and re-layouts  0.7 us (1%)
    pallas_call x1, Pallas kernels, local(): pl.pallas_call(kernel, out_shape=VMEM((JL, ROWS, NLON), BF16), in_specs=[...  49.7 us

profile of v3, /device:TPU:1, one launch (start us, length us, event | category | flops | bytes accessed | tf_op | source)
XLA Modules:
  0.0 50.4 jit_solution(18390276693516448020)
XLA Ops:
  0.0 49.7 %transform_step.1 = bf16[30,4,1024]{2,1,0:T(4,128)(2,1)S(1)} custom-call(s32[480]{0:T(512)} %lat_hbm.1, f32[480]{0:T(512)} %gauss_hbm.1, s32[160]{0:T(256)} %pair_hbm.1, s32[1,480]{1,0:T(1,128)} %bitcast.8, s32[1,160]{1,0:T(1,128)} %bitcast.9, s32[1,256]{1,0:T(1,128)} %bitcast.10, f32[1,128]{1,0:T(1,128)} %bitcast.11, bf16[128,128]{1,0:T(8,128)(2,1)} %modes_in_hbm.1, ...), custom_call_target="tpu_custom_call" | custom-call | tf_op jit(solution)/shard_map/transform_step/pallas_call | solution.py:357
  49.7 0.7 %copy.12 = bf16[4,30,1024]{2,0,1:T(4,128)(2,1)} copy(bf16[4,30,1024]{2,0,1:T(4,128)(2,1)S(1)} %bitcast.6) | data formatting | bytes 491520

commit v4 on v3

--- a/solution.py
+++ b/solution.py
@@ -96,11 +96,11 @@
 def enter():
     barrier = pltpu.get_barrier_semaphore()
     xs, ys = lev_places()
+    for to in wave_partners():
+        signal(barrier, "wave", to)
     for step in RING_STEPS:
         signal(barrier, "lev", xs[step] + ys[0])
         signal(barrier, "lev", xs[0] + ys[step])
-    for to in wave_partners():
-        signal(barrier, "wave", to)
 
 
 def pass_on(semaphore):
@@ -166,21 +166,21 @@
     recv_buf[w] = send_buf[w]
 
 
-def send_lev(send_buf, recv_buf, send_sem, recv_sem, limit):
-    me = lax.axis_index("lev")
-    for to in lev_partners():
-        copy = pltpu.make_async_remote_copy(
-            src_ref=send_buf.at[to],
-            dst_ref=recv_buf.at[me],
-            send_sem=send_sem,
-            recv_sem=recv_sem,
-            device_id={"lev": to},
-            device_id_type=MESH,
-        )
-        if limit == LV:
-            copy.start()
-        else:
-            pl.when(to < limit)(copy.start)
+def lev_copy(send_buf, recv_buf, send_sem, recv_sem, to):
+    return pltpu.make_async_remote_copy(
+        src_ref=send_buf.at[to],
+        dst_ref=recv_buf.at[lax.axis_index("lev")],
+        send_sem=send_sem,
+        recv_sem=recv_sem,
+        device_id={"lev": to},
+        device_id_type=MESH,
+    )
+
+
+def slots_by_distance():
+    x = lax.div(lax.axis_index("lev"), 8)
+    own = lax.min(lax.div(8 * x + 3, 6), SLOTS - 1)
+    return [lax.rem(own + step, SLOTS) for step in (5, 4, 6, 3, 7, 2, 8, 1, 9, 0)]
 
 
 def kernel(
@@ -189,7 +189,7 @@
     lat_s, gauss_s, pair_s, lat_v, pair_v, slots_v, stiff_v, modes_in_v, modes_out_v, grid_v,
     table_v, basis, spread, send_a, recv_a, mixed, degrees, selector, slot_order, slot_table, modes_a,
     modes_b, factor_v, out_b, in_b, back_b, home_b, rows_f, send_c, recv_c, slotted,
-    copy_sem, send_sem, recv_sem, ring_sem,
+    copy_sem, send_sem, recv_sem, home_sem, ring_sem,
 ):
     w = lax.axis_index("wave")
     me = lax.axis_index("lev")
@@ -258,17 +258,28 @@
             mixed[g, pl.ds(r, 40, stride=ROWS), :] = pieces[r]
     degrees[...] = dot_nt(joined(mixed).astype(BF16), selector[...]).astype(BF16)
     all_columns = iota((8, COLS), 1)
-    firsts = [all_columns < NM - pair_s[w * SLOTS + k] for k in range(SLOTS)]
-    for k in range(SLOTS):
-        both = dot(degrees[16 * k : 16 * k + 16], basis[k])
-        picked = jnp.where(firsts[k], both[0:8], both[8:16])
+    order = slots_by_distance()
+
+    def send_blocks(k):
+        for j in range(6):
+            copy = lev_copy(out_b, in_b, send_sem.at[1], recv_sem.at[1], 6 * k + j)
+            pl.when(6 * k + j != me)(copy.start)
+
+    pl.semaphore_wait(ring_sem, 7)
+    before = None
+    for k in order:
+        both = dot(degrees[pl.ds(pl.multiple_of(16 * k, 16), 16)], basis[k])
+        first = all_columns < NM - pair_s[w * SLOTS + k]
+        picked = jnp.where(first, both[0:8], both[8:16])
         for q in range(2):
             for c in range(3):
-                out_b[6 * k + 3 * q + c] = picked[
+                out_b[6 * k + (3 * q + c)] = picked[
                     4 * q : 4 * q + 4, 128 * c : 128 * c + 128
                 ].astype(BF16)
-    pl.semaphore_wait(ring_sem, 7)
-    send_lev(out_b, in_b, send_sem.at[1], recv_sem.at[1], NB)
+        if before is not None:
+            send_blocks(before)
+        before = k
+    send_blocks(before)
 
     for b in range(5):
         part = pl.ds(128 * b, 128)
@@ -286,28 +297,29 @@
         rows_f[...] = dot(modes_b[...], modal.astype(BF16))
         for s in range(LV):
             back_b[s] = rows_f[4 * s : 4 * s + 4].astype(BF16)
-        send_lev(back_b, home_b, send_sem.at[2], recv_sem.at[2], LV)
+        for to in lev_partners():
+            lev_copy(back_b, home_b, send_sem.at[2], home_sem.at[lax.div(me, 6)], to).start()
         home_b[me] = back_b[me]
-        wait_bytes(home_b, NB - 1, recv_sem.at[2])
-
-    @pl.when(jnp.logical_not(works))
-    def _():
-        wait_bytes(home_b, NB, recv_sem.at[2])
-
-    for k in range(SLOTS):
+
+    for k in reversed(order):
+        own = lax.div(me, 6) == k
+        pl.when(own)(lambda k=k: wait_bytes(home_b, 5, home_sem.at[k]))
+        pl.when(jnp.logical_not(own))(lambda k=k: wait_bytes(home_b, 6, home_sem.at[k]))
         values = jnp.concatenate(
             [
                 jnp.concatenate(
-                    [home_b[6 * k + 3 * q + c].astype(F32) for c in range(3)], axis=1
+                    [home_b[6 * k + (3 * q + c)].astype(F32) for c in range(3)], axis=1
                 )
                 for q in range(2)
             ],
             axis=0,
         )
+        first = all_columns < NM - pair_s[w * SLOTS + k]
         both = jnp.concatenate(
-            [jnp.where(firsts[k], values, 0.0), jnp.where(firsts[k], 0.0, values)], axis=0
+            [jnp.where(first, values, 0.0), jnp.where(first, 0.0, values)], axis=0
         )
-        degrees[16 * k : 16 * k + 16] = dot_nt(both.astype(BF16), basis[k]).astype(BF16)
+        back = dot_nt(both.astype(BF16), basis[k]).astype(BF16)
+        degrees[pl.ds(pl.multiple_of(16 * k, 16), 16)] = back
     there = dot(degrees[...], selector[...])
     for g in range(4):
         mixed[g] = there[:, 128 * g : 128 * g + 128]
@@ -394,6 +406,7 @@
             DMA((12,)),
             DMA((4,)),
             DMA((4,)),
+            DMA((SLOTS,)),
             pltpu.SemaphoreType.REGULAR,
         ],
         compiler_params=pltpu.CompilerParams(

time: 50.6 us -> 51.6 us (1.020)
  Pallas kernels: 49.7 us -> 50.8 us
    pallas_call x1, Pallas kernels: 49.7 us -> 50.8 us  [local(): pl.pallas_call(kernel, out_shape=VMEM((JL, ROWS, NLON), BF16), in_specs=[...]
where the time goes in v4:
time: 51.6 us; the launch traced here: 51.5 us
  Pallas kernels  50.8 us (98%)
  local copies, waits for them, and re-layouts  0.7 us (1%)
    pallas_call x1, Pallas kernels, local(): pl.pallas_call(kernel, out_shape=VMEM((JL, ROWS, NLON), BF16), in_specs=[...  50.8 us

profile of v4, /device:TPU:1, one launch (start us, length us, event | category | flops | bytes accessed | tf_op | source)
XLA Modules:
  0.0 51.5 jit_solution(2235544412060246412)
XLA Ops:
  0.0 50.8 %transform_step.1 = bf16[30,4,1024]{2,1,0:T(4,128)(2,1)S(1)} custom-call(s32[480]{0:T(512)} %lat_hbm.1, f32[480]{0:T(512)} %gauss_hbm.1, s32[160]{0:T(256)} %pair_hbm.1, s32[1,480]{1,0:T(1,128)} %bitcast.8, s32[1,160]{1,0:T(1,128)} %bitcast.9, s32[1,256]{1,0:T(1,128)} %bitcast.10, f32[1,128]{1,0:T(1,128)} %bitcast.11, bf16[128,128]{1,0:T(8,128)(2,1)} %modes_in_hbm.1, ...), custom_call_target="tpu_custom_call" | custom-call | tf_op jit(solution)/shard_map/transform_step/pallas_call | solution.py:369
  50.8 0.7 %copy.12 = bf16[4,30,1024]{2,0,1:T(4,128)(2,1)} copy(bf16[4,30,1024]{2,0,1:T(4,128)(2,1)S(1)} %bitcast.6) | data formatting | bytes 491520

commit v5 on v3

--- a/solution.py
+++ b/solution.py
@@ -20,6 +20,7 @@
 COLS = 384
 NB = 60
 NLON = 1024
+PARTS = ((0, 4), (4, SLOTS))
 F32 = jnp.float32
 BF16 = jnp.bfloat16
 MESH = pl.DeviceIdType.MESH
@@ -187,13 +188,17 @@
     lat_hbm, gauss_hbm, pair_hbm, lat_row, pair_row, slots_row, stiff_row, modes_in_hbm,
     modes_out_hbm, grid_hbm, table_hbm, basis_hbm, out_ref,
     lat_s, gauss_s, pair_s, lat_v, pair_v, slots_v, stiff_v, modes_in_v, modes_out_v, grid_v,
-    table_v, basis, spread, send_a, recv_a, mixed, degrees, selector, slot_order, slot_table, modes_a,
-    modes_b, factor_v, out_b, in_b, back_b, home_b, rows_f, send_c, recv_c, slotted,
+    table_v, basis, spread, send_a0, send_a1, recv_a0, recv_a1, mixed, degrees, selector, slot_order,
+    slot_table0, slot_table1, modes_a, modes_b, factor_v, out_b, in_b, back_b, home_b, rows_f,
+    send_c0, send_c1, recv_c0, recv_c1, slotted, fields_v,
     copy_sem, send_sem, recv_sem, ring_sem,
 ):
     w = lax.axis_index("wave")
     me = lax.axis_index("lev")
     works = me < NB
+    send_a, recv_a = (send_a0, send_a1), (recv_a0, recv_a1)
+    send_c, recv_c = (send_c0, send_c1), (recv_c0, recv_c1)
+    slot_table = (slot_table0, slot_table1)
     pairs = [
         (grid_hbm, grid_v), (pair_row, pair_v), (lat_hbm, lat_s), (gauss_hbm, gauss_s),
         (table_hbm, table_v), (pair_hbm, pair_s), (lat_row, lat_v), (slots_row, slots_v),
@@ -227,10 +232,12 @@
     fourier = (dot_nt(table_v[...], values) * weight).astype(BF16)
     slots = dot(slot_order[...], fourier)
     for d in range(W):
-        send_a[d] = slots[40 * d : 40 * d + 40].astype(BF16)
+        for part, (start, end) in enumerate(PARTS):
+            send_a[part][d] = slots[40 * d + 4 * start : 40 * d + 4 * end].astype(BF16)
     pl.semaphore_wait(pltpu.get_barrier_semaphore(), W - 1 + 14)
     pass_on(ring_sem)
-    send_wave(send_a, recv_a, send_sem.at[0], recv_sem.at[0])
+    for part in range(2):
+        send_wave(send_a[part], recv_a[part], send_sem.at[part], recv_sem.at[part])
 
     for get in gets[5:11]:
         get.wait()
@@ -251,33 +258,43 @@
     factor_v[...] = 1.0 / (1.0 + growth * stiffness)
     gets[11].wait()
 
-    wait_bytes(recv_a, W - 1, recv_sem.at[0])
-    for g in range(4):
-        pieces = rows_to_lanes([recv_a[4 * g + s].astype(F32) for s in range(4)])
-        for r in range(ROWS):
-            mixed[g, pl.ds(r, 40, stride=ROWS), :] = pieces[r]
-    degrees[...] = dot_nt(joined(mixed).astype(BF16), selector[...]).astype(BF16)
     all_columns = iota((8, COLS), 1)
     firsts = [all_columns < NM - pair_s[w * SLOTS + k] for k in range(SLOTS)]
-    for k in range(SLOTS):
-        both = dot(degrees[16 * k : 16 * k + 16], basis[k])
-        picked = jnp.where(firsts[k], both[0:8], both[8:16])
-        for q in range(2):
-            for c in range(3):
-                out_b[6 * k + 3 * q + c] = picked[
-                    4 * q : 4 * q + 4, 128 * c : 128 * c + 128
-                ].astype(BF16)
+    for part, (start, end) in enumerate(PARTS):
+        wait_bytes(recv_a[part], W - 1, recv_sem.at[part])
+        count = 4 * (end - start)
+        rows = slice(16 * start, 16 * end)
+        for g in range(4):
+            pieces = rows_to_lanes(
+                [recv_a[part][4 * g + s].astype(F32) for s in range(4)]
+            )
+            for r in range(ROWS):
+                mixed[g, pl.ds(16 * start + r, count, stride=ROWS), :] = pieces[r]
+        values = jnp.concatenate([mixed[g, rows] for g in range(4)], axis=1)
+        degrees[rows] = dot_nt(values.astype(BF16), selector[...]).astype(BF16)
+        for k in range(start, end):
+            both = dot(degrees[16 * k : 16 * k + 16], basis[k])
+            picked = jnp.where(firsts[k], both[0:8], both[8:16])
+            for q in range(2):
+                for c in range(3):
+                    out_b[6 * k + 3 * q + c] = picked[
+                        4 * q : 4 * q + 4, 128 * c : 128 * c + 128
+                    ].astype(BF16)
     pl.semaphore_wait(ring_sem, 7)
-    send_lev(out_b, in_b, send_sem.at[1], recv_sem.at[1], NB)
-
-    for b in range(5):
-        part = pl.ds(128 * b, 128)
-        slot_table[part] = dot(slot_order[part], table_v[...]).astype(BF16)
+    send_lev(out_b, in_b, send_sem.at[2], recv_sem.at[2], NB)
+
+    for pair in range(W // 2):
+        rows = dot(slot_order[80 * pair : 80 * pair + 80], table_v[...])
+        for part, (start, end) in enumerate(PARTS):
+            count = 8 * (end - start)
+            picked = [rows[40 * d + 4 * start : 40 * d + 4 * end] for d in range(2)]
+            picked = jnp.concatenate(picked, axis=0).astype(BF16)
+            slot_table[part][count * pair : count * pair + count] = picked
 
     @pl.when(works)
     def _():
         in_b[me] = out_b[me]
-        wait_bytes(in_b, LV - 1, recv_sem.at[1])
+        wait_bytes(in_b, LV - 1, recv_sem.at[2])
         for s in range(LV):
             rows_f[4 * s : 4 * s + 4] = in_b[s].astype(F32)
         modal = dot(modes_a[...], rows_f[...].astype(BF16))
@@ -286,61 +303,72 @@
         rows_f[...] = dot(modes_b[...], modal.astype(BF16))
         for s in range(LV):
             back_b[s] = rows_f[4 * s : 4 * s + 4].astype(BF16)
-        send_lev(back_b, home_b, send_sem.at[2], recv_sem.at[2], LV)
+        send_lev(back_b, home_b, send_sem.at[3], recv_sem.at[3], LV)
         home_b[me] = back_b[me]
-        wait_bytes(home_b, NB - 1, recv_sem.at[2])
+        wait_bytes(home_b, NB - 1, recv_sem.at[3])
 
     @pl.when(jnp.logical_not(works))
     def _():
-        wait_bytes(home_b, NB, recv_sem.at[2])
-
-    for k in range(SLOTS):
-        values = jnp.concatenate(
-            [
-                jnp.concatenate(
-                    [home_b[6 * k + 3 * q + c].astype(F32) for c in range(3)], axis=1
-                )
-                for q in range(2)
-            ],
-            axis=0,
-        )
-        both = jnp.concatenate(
-            [jnp.where(firsts[k], values, 0.0), jnp.where(firsts[k], 0.0, values)], axis=0
-        )
-        degrees[16 * k : 16 * k + 16] = dot_nt(both.astype(BF16), basis[k]).astype(BF16)
-    there = dot(degrees[...], selector[...])
-    for g in range(4):
-        mixed[g] = there[:, 128 * g : 128 * g + 128]
-    for g in range(4):
-        pieces = rows_to_lanes(
-            [mixed[g, pl.ds(r, 40, stride=ROWS), :] for r in range(ROWS)]
-        )
-        for s in range(4):
-            send_c[4 * g + s] = pieces[s].astype(BF16)
-    send_wave(send_c, recv_c, send_sem.at[3], recv_sem.at[3])
+        wait_bytes(home_b, NB, recv_sem.at[3])
+
+    for part, (start, end) in enumerate(PARTS):
+        for k in range(start, end):
+            values = jnp.concatenate(
+                [
+                    jnp.concatenate(
+                        [home_b[6 * k + 3 * q + c].astype(F32) for c in range(3)], axis=1
+                    )
+                    for q in range(2)
+                ],
+                axis=0,
+            )
+            both = jnp.concatenate(
+                [jnp.where(firsts[k], values, 0.0), jnp.where(firsts[k], 0.0, values)], axis=0
+            )
+            degrees[16 * k : 16 * k + 16] = dot_nt(both.astype(BF16), basis[k]).astype(BF16)
+        rows = slice(16 * start, 16 * end)
+        there = dot(degrees[rows], selector[...])
+        for g in range(4):
+            mixed[g, rows] = there[:, 128 * g : 128 * g + 128]
+        count = 4 * (end - start)
+        for g in range(4):
+            pieces = rows_to_lanes(
+                [mixed[g, pl.ds(16 * start + r, count, stride=ROWS), :] for r in range(ROWS)]
+            )
+            for s in range(4):
+                send_c[part][4 * g + s] = pieces[s].astype(BF16)
+        send_wave(send_c[part], recv_c[part], send_sem.at[4 + part], recv_sem.at[4 + part])
 
     @pl.when(works)
     def _():
-        wait_bytes(out_b, NB - 1, send_sem.at[1])
-        wait_bytes(back_b, LV - 1, send_sem.at[2])
+        wait_bytes(out_b, NB - 1, send_sem.at[2])
+        wait_bytes(back_b, LV - 1, send_sem.at[3])
 
     @pl.when(jnp.logical_not(works))
     def _():
-        wait_bytes(out_b, NB, send_sem.at[1])
-
-    wait_bytes(send_a, W - 1, send_sem.at[0])
-
-    wait_bytes(recv_c, W - 1, recv_sem.at[3])
-    for d in range(W):
-        slotted[40 * d : 40 * d + 40] = recv_c[d].astype(F32)
-    fields = dot(jnp.transpose(slotted[...]).astype(BF16), slot_table[...])
+        wait_bytes(out_b, NB, send_sem.at[2])
+
+    for part in range(2):
+        wait_bytes(send_a[part], W - 1, send_sem.at[part])
+
+    for part, (start, end) in enumerate(PARTS):
+        wait_bytes(recv_c[part], W - 1, recv_sem.at[4 + part])
+        count = 4 * (end - start)
+        for d in range(W):
+            slotted[count * d : count * d + count] = recv_c[part][d].astype(F32)
+        values = jnp.transpose(slotted[: W * count]).astype(BF16)
+        fields = dot(values, slot_table[part][...])
+        if part == 0:
+            fields_v[...] = fields
+    fields = fields_v[...] + fields
     for b in range(8):
         spread[b] = spread[b] * fields[:, 128 * b : 128 * b + 128]
     for jl in range(JL):
         for b in range(8):
             rows = spread[b, pl.ds(jl, ROWS, stride=JP), :]
             out_ref[jl, :, 128 * b : 128 * b + 128] = rows.astype(BF16)
-    wait_bytes(send_c, W - 1, send_sem.at[3])
+    for part in range(2):
+        wait_bytes(send_c[part], W - 1, send_sem.at[4 + part])
 
 
 def local(
@@ -373,13 +401,16 @@
             VMEM((640, NLON), BF16),
             VMEM((SLOTS, LAT, COLS), BF16),
             VMEM((8, 128, 128), F32),
-            VMEM((W, 40, 128), BF16),
-            VMEM((W, 40, 128), BF16),
+            VMEM((W, 16, 128), BF16),
+            VMEM((W, 24, 128), BF16),
+            VMEM((W, 16, 128), BF16),
+            VMEM((W, 24, 128), BF16),
             VMEM((4, 160, 128), F32),
             VMEM((160, LAT), BF16),
             VMEM((LAT, W * JP), BF16),
             VMEM((640, 640), BF16),
-            VMEM((640, NLON), BF16),
+            VMEM((256, NLON), BF16),
+            VMEM((384, NLON), BF16),
             VMEM((256, 256), BF16),
             VMEM((256, 256), BF16),
             VMEM((LEVELS, 128), F32),
@@ -388,12 +419,15 @@
             VMEM((LV, ROWS, 128), BF16),
             VMEM((NB, ROWS, 128), BF16),
             VMEM((256, 128), F32),
-            VMEM((W, 40, 128), BF16),
-            VMEM((W, 40, 128), BF16),
-            VMEM((640, 128), F32),
+            VMEM((W, 16, 128), BF16),
+            VMEM((W, 24, 128), BF16),
+            VMEM((W, 16, 128), BF16),
+            VMEM((W, 24, 128), BF16),
+            VMEM((384, 128), F32),
+            VMEM((128, NLON), F32),
             DMA((12,)),
-            DMA((4,)),
-            DMA((4,)),
+            DMA((6,)),
+            DMA((6,)),
             pltpu.SemaphoreType.REGULAR,
         ],
         compiler_params=pltpu.CompilerParams(

time: 50.6 us -> 51 us (level)
  no operation moved by 1% of the time
where the time goes in v5:
time: 51 us; the launch traced here: 50.8 us
  Pallas kernels  50.1 us (98%)
  local copies, waits for them, and re-layouts  0.7 us (1%)
    pallas_call x1, Pallas kernels, local(): pl.pallas_call(kernel, out_shape=VMEM((JL, ROWS, NLON), BF16), in_specs=[...  50.1 us

profile of v5, /device:TPU:1, one launch (start us, length us, event | category | flops | bytes accessed | tf_op | source)
XLA Modules:
  0.0 50.8 jit_solution(7355491078972044469)
XLA Ops:
  0.0 50.1 %transform_step.1 = bf16[30,4,1024]{2,1,0:T(4,128)(2,1)S(1)} custom-call(s32[480]{0:T(512)} %lat_hbm.1, f32[480]{0:T(512)} %gauss_hbm.1, s32[160]{0:T(256)} %pair_hbm.1, s32[1,480]{1,0:T(1,128)} %bitcast.8, s32[1,160]{1,0:T(1,128)} %bitcast.9, s32[1,256]{1,0:T(1,128)} %bitcast.10, f32[1,128]{1,0:T(1,128)} %bitcast.11, bf16[128,128]{1,0:T(8,128)(2,1)} %modes_in_hbm.1, ...), custom_call_target="tpu_custom_call" | custom-call | tf_op jit(solution)/shard_map/transform_step/pallas_call | solution.py:385
  50.1 0.7 %copy.12 = bf16[4,30,1024]{2,0,1:T(4,128)(2,1)} copy(bf16[4,30,1024]{2,0,1:T(4,128)(2,1)S(1)} %bitcast.6) | data formatting | bytes 491520

commit v6 on v3

--- a/solution.py
+++ b/solution.py
@@ -96,11 +96,11 @@
 def enter():
     barrier = pltpu.get_barrier_semaphore()
     xs, ys = lev_places()
+    for to in wave_partners():
+        signal(barrier, "wave", to)
     for step in RING_STEPS:
         signal(barrier, "lev", xs[step] + ys[0])
         signal(barrier, "lev", xs[0] + ys[step])
-    for to in wave_partners():
-        signal(barrier, "wave", to)
 
 
 def pass_on(semaphore):
@@ -188,7 +188,7 @@
     modes_out_hbm, grid_hbm, table_hbm, basis_hbm, out_ref,
     lat_s, gauss_s, pair_s, lat_v, pair_v, slots_v, stiff_v, modes_in_v, modes_out_v, grid_v,
     table_v, basis, spread, send_a, recv_a, mixed, degrees, selector, slot_order, slot_table, modes_a,
-    modes_b, factor_v, out_b, in_b, back_b, home_b, rows_f, send_c, recv_c, slotted,
+    modes_b, factor_v, out_b, in_b, back_b, home_b, rows_f, send_c, recv_c, slotted, grid_f,
     copy_sem, send_sem, recv_sem, ring_sem,
 ):
     w = lax.axis_index("wave")
@@ -273,6 +273,9 @@
     for b in range(5):
         part = pl.ds(128 * b, 128)
         slot_table[part] = dot(slot_order[part], table_v[...]).astype(BF16)
+
+    for jl in range(JL):
+        grid_f[4 * jl : 4 * jl + 4] = grid_v[jl].astype(F32)
 
     @pl.when(works)
     def _():
@@ -333,13 +336,13 @@
     wait_bytes(recv_c, W - 1, recv_sem.at[3])
     for d in range(W):
         slotted[40 * d : 40 * d + 40] = recv_c[d].astype(F32)
-    fields = dot(jnp.transpose(slotted[...]).astype(BF16), slot_table[...])
-    for b in range(8):
-        spread[b] = spread[b] * fields[:, 128 * b : 128 * b + 128]
+    point = iota((JL * ROWS, 128), 0)
+    lanes = (point & 3) * JP + (point >> 2)
+    to_points = one_hot(iota((JL * ROWS, 128), 1) == lanes)
+    by_point = dot_nt(to_points, slotted[...].astype(BF16)).astype(BF16)
+    products = dot(by_point, slot_table[...]) * grid_f[...]
     for jl in range(JL):
-        for b in range(8):
-            rows = spread[b, pl.ds(jl, ROWS, stride=JP), :]
-            out_ref[jl, :, 128 * b : 128 * b + 128] = rows.astype(BF16)
+        out_ref[jl] = products[4 * jl : 4 * jl + 4].astype(BF16)
     wait_bytes(send_c, W - 1, send_sem.at[3])
 
 
@@ -391,6 +394,7 @@
             VMEM((W, 40, 128), BF16),
             VMEM((W, 40, 128), BF16),
             VMEM((640, 128), F32),
+            VMEM((JL * ROWS, NLON), F32),
             DMA((12,)),
             DMA((4,)),
             DMA((4,)),

time: 50.6 us -> 50.4 us (level)
  no operation moved by 1% of the time
where the time goes in v6:
time: 50.4 us; the launch traced here: 50.3 us
  Pallas kernels  49.6 us (98%)
  local copies, waits for them, and re-layouts  0.7 us (1%)
    pallas_call x1, Pallas kernels, local(): pl.pallas_call(kernel, out_shape=VMEM((JL, ROWS, NLON), BF16), in_specs=[...  49.6 us

profile of v6, /device:TPU:1, one launch (start us, length us, event | category | flops | bytes accessed | tf_op | source)
XLA Modules:
  0.0 50.3 jit_solution(15445586606800569800)
XLA Ops:
  0.0 49.6 %transform_step.1 = bf16[30,4,1024]{2,1,0:T(4,128)(2,1)S(1)} custom-call(s32[480]{0:T(512)} %lat_hbm.1, f32[480]{0:T(512)} %gauss_hbm.1, s32[160]{0:T(256)} %pair_hbm.1, s32[1,480]{1,0:T(1,128)} %bitcast.8, s32[1,160]{1,0:T(1,128)} %bitcast.9, s32[1,256]{1,0:T(1,128)} %bitcast.10, f32[1,128]{1,0:T(1,128)} %bitcast.11, bf16[128,128]{1,0:T(8,128)(2,1)} %modes_in_hbm.1, ...), custom_call_target="tpu_custom_call" | custom-call | tf_op jit(solution)/shard_map/transform_step/pallas_call | solution.py:360
  49.6 0.7 %copy.12 = bf16[4,30,1024]{2,0,1:T(4,128)(2,1)} copy(bf16[4,30,1024]{2,0,1:T(4,128)(2,1)S(1)} %bitcast.6) | data formatting | bytes 491520

commit v7 on v6

--- a/solution.py
+++ b/solution.py
@@ -20,6 +20,7 @@
 COLS = 384
 NB = 60
 NLON = 1024
+PARTS = ((0, 4), (4, SLOTS))
 F32 = jnp.float32
 BF16 = jnp.bfloat16
 MESH = pl.DeviceIdType.MESH
@@ -166,34 +167,29 @@
     recv_buf[w] = send_buf[w]
 
 
-def send_lev(send_buf, recv_buf, send_sem, recv_sem, limit):
-    me = lax.axis_index("lev")
-    for to in lev_partners():
-        copy = pltpu.make_async_remote_copy(
-            src_ref=send_buf.at[to],
-            dst_ref=recv_buf.at[me],
-            send_sem=send_sem,
-            recv_sem=recv_sem,
-            device_id={"lev": to},
-            device_id_type=MESH,
-        )
-        if limit == LV:
-            copy.start()
-        else:
-            pl.when(to < limit)(copy.start)
+def lev_copy(send_buf, recv_buf, send_sem, recv_sem, to):
+    return pltpu.make_async_remote_copy(
+        src_ref=send_buf.at[to],
+        dst_ref=recv_buf.at[lax.axis_index("lev")],
+        send_sem=send_sem,
+        recv_sem=recv_sem,
+        device_id={"lev": to},
+        device_id_type=MESH,
+    )
 
 
 def kernel(
     lat_hbm, gauss_hbm, pair_hbm, lat_row, pair_row, slots_row, stiff_row, modes_in_hbm,
     modes_out_hbm, grid_hbm, table_hbm, basis_hbm, out_ref,
     lat_s, gauss_s, pair_s, lat_v, pair_v, slots_v, stiff_v, modes_in_v, modes_out_v, grid_v,
-    table_v, basis, spread, send_a, recv_a, mixed, degrees, selector, slot_order, slot_table, modes_a,
+    table_v, basis, spread, send_a0, send_a1, recv_a0, recv_a1, mixed, degrees, selector, slot_order, slot_table, modes_a,
     modes_b, factor_v, out_b, in_b, back_b, home_b, rows_f, send_c, recv_c, slotted, grid_f,
     copy_sem, send_sem, recv_sem, ring_sem,
 ):
     w = lax.axis_index("wave")
     me = lax.axis_index("lev")
     works = me < NB
+    send_a, recv_a = (send_a0, send_a1), (recv_a0, recv_a1)
     pairs = [
         (grid_hbm, grid_v), (pair_row, pair_v), (lat_hbm, lat_s), (gauss_hbm, gauss_s),
         (table_hbm, table_v), (pair_hbm, pair_s), (lat_row, lat_v), (slots_row, slots_v),
@@ -227,10 +223,12 @@
     fourier = (dot_nt(table_v[...], values) * weight).astype(BF16)
     slots = dot(slot_order[...], fourier)
     for d in range(W):
-        send_a[d] = slots[40 * d : 40 * d + 40].astype(BF16)
+        for part, (start, end) in enumerate(PARTS):
+            send_a[part][d] = slots[40 * d + 4 * start : 40 * d + 4 * end].astype(BF16)
     pl.semaphore_wait(pltpu.get_barrier_semaphore(), W - 1 + 14)
     pass_on(ring_sem)
-    send_wave(send_a, recv_a, send_sem.at[0], recv_sem.at[0])
+    for part in range(2):
+        send_wave(send_a[part], recv_a[part], send_sem.at[4 * part], recv_sem.at[4 * part])
 
     for get in gets[5:11]:
         get.wait()
@@ -251,24 +249,37 @@
     factor_v[...] = 1.0 / (1.0 + growth * stiffness)
     gets[11].wait()
 
-    wait_bytes(recv_a, W - 1, recv_sem.at[0])
-    for g in range(4):
-        pieces = rows_to_lanes([recv_a[4 * g + s].astype(F32) for s in range(4)])
-        for r in range(ROWS):
-            mixed[g, pl.ds(r, 40, stride=ROWS), :] = pieces[r]
-    degrees[...] = dot_nt(joined(mixed).astype(BF16), selector[...]).astype(BF16)
     all_columns = iota((8, COLS), 1)
     firsts = [all_columns < NM - pair_s[w * SLOTS + k] for k in range(SLOTS)]
-    for k in range(SLOTS):
-        both = dot(degrees[16 * k : 16 * k + 16], basis[k])
-        picked = jnp.where(firsts[k], both[0:8], both[8:16])
-        for q in range(2):
-            for c in range(3):
-                out_b[6 * k + 3 * q + c] = picked[
-                    4 * q : 4 * q + 4, 128 * c : 128 * c + 128
-                ].astype(BF16)
-    pl.semaphore_wait(ring_sem, 7)
-    send_lev(out_b, in_b, send_sem.at[1], recv_sem.at[1], NB)
+    for part, (start, end) in enumerate(PARTS):
+        wait_bytes(recv_a[part], W - 1, recv_sem.at[4 * part])
+        count = 4 * (end - start)
+        rows = slice(16 * start, 16 * end)
+        for g in range(4):
+            pieces = rows_to_lanes(
+                [recv_a[part][4 * g + s].astype(F32) for s in range(4)]
+            )
+            for r in range(ROWS):
+                mixed[g, pl.ds(16 * start + r, count, stride=ROWS), :] = pieces[r]
+        values = jnp.concatenate([mixed[g, rows] for g in range(4)], axis=1)
+        degrees[rows] = dot_nt(values.astype(BF16), selector[...]).astype(BF16)
+        for k in range(start, end):
+            both = dot(degrees[16 * k : 16 * k + 16], basis[k])
+            picked = jnp.where(firsts[k], both[0:8], both[8:16])
+            for q in range(2):
+                for c in range(3):
+                    out_b[6 * k + 3 * q + c] = picked[
+                        4 * q : 4 * q + 4, 128 * c : 128 * c + 128
+                    ].astype(BF16)
+        if part == 0:
+            pl.semaphore_wait(ring_sem, 7)
+            for to in range(6 * end):
+                copy = lev_copy(out_b, in_b, send_sem.at[1], recv_sem.at[1], to)
+                pl.when(to != me)(copy.start)
+        else:
+            for to in lev_partners():
+                copy = lev_copy(out_b, in_b, send_sem.at[1], recv_sem.at[1], to)
+                pl.when(jnp.logical_and(to >= 6 * start, to < NB))(copy.start)
 
     for b in range(5):
         part = pl.ds(128 * b, 128)
@@ -289,7 +300,8 @@
         rows_f[...] = dot(modes_b[...], modal.astype(BF16))
         for s in range(LV):
             back_b[s] = rows_f[4 * s : 4 * s + 4].astype(BF16)
-        send_lev(back_b, home_b, send_sem.at[2], recv_sem.at[2], LV)
+        for to in lev_partners():
+            lev_copy(back_b, home_b, send_sem.at[2], recv_sem.at[2], to).start()
         home_b[me] = back_b[me]
         wait_bytes(home_b, NB - 1, recv_sem.at[2])
 
@@ -331,7 +343,8 @@
     def _():
         wait_bytes(out_b, NB, send_sem.at[1])
 
-    wait_bytes(send_a, W - 1, send_sem.at[0])
+    for part in range(2):
+        wait_bytes(send_a[part], W - 1, send_sem.at[4 * part])
 
     wait_bytes(recv_c, W - 1, recv_sem.at[3])
     for d in range(W):
@@ -376,8 +389,10 @@
             VMEM((640, NLON), BF16),
             VMEM((SLOTS, LAT, COLS), BF16),
             VMEM((8, 128, 128), F32),
-            VMEM((W, 40, 128), BF16),
-            VMEM((W, 40, 128), BF16),
+            VMEM((W, 16, 128), BF16),
+            VMEM((W, 24, 128), BF16),
+            VMEM((W, 16, 128), BF16),
+            VMEM((W, 24, 128), BF16),
             VMEM((4, 160, 128), F32),
             VMEM((160, LAT), BF16),
             VMEM((LAT, W * JP), BF16),
@@ -396,8 +411,8 @@
             VMEM((640, 128), F32),
             VMEM((JL * ROWS, NLON), F32),
             DMA((12,)),
-            DMA((4,)),
-            DMA((4,)),
+            DMA((5,)),
+            DMA((5,)),
             pltpu.SemaphoreType.REGULAR,
         ],
         compiler_params=pltpu.CompilerParams(

time: 50.4 us -> 51 us (1.012)
  Pallas kernels: 49.6 us -> 50.2 us
    pallas_call x1, Pallas kernels: 49.6 us -> 50.2 us  [local(): pl.pallas_call(kernel, out_shape=VMEM((JL, ROWS, NLON), BF16), in_specs=[...]
where the time goes in v7:
time: 51 us; the launch traced here: 50.9 us
  Pallas kernels  50.2 us (98%)
  local copies, waits for them, and re-layouts  0.7 us (1%)
    pallas_call x1, Pallas kernels, local(): pl.pallas_call(kernel, out_shape=VMEM((JL, ROWS, NLON), BF16), in_specs=[...  50.2 us

profile of v7, /device:TPU:1, one launch (start us, length us, event | category | flops | bytes accessed | tf_op | source)
XLA Modules:
  0.0 50.9 jit_solution(15918025824649461587)
XLA Ops:
  0.0 50.2 %transform_step.1 = bf16[30,4,1024]{2,1,0:T(4,128)(2,1)S(1)} custom-call(s32[480]{0:T(512)} %lat_hbm.1, f32[480]{0:T(512)} %gauss_hbm.1, s32[160]{0:T(256)} %pair_hbm.1, s32[1,480]{1,0:T(1,128)} %bitcast.8, s32[1,160]{1,0:T(1,128)} %bitcast.9, s32[1,256]{1,0:T(1,128)} %bitcast.10, f32[1,128]{1,0:T(1,128)} %bitcast.11, bf16[128,128]{1,0:T(8,128)(2,1)} %modes_in_hbm.1, ...), custom_call_target="tpu_custom_call" | custom-call | tf_op jit(solution)/shard_map/transform_step/pallas_call | solution.py:373
  50.2 0.7 %copy.12 = bf16[4,30,1024]{2,0,1:T(4,128)(2,1)} copy(bf16[4,30,1024]{2,0,1:T(4,128)(2,1)S(1)} %bitcast.6) | data formatting | bytes 491520
